TPU v7x, 32 devices: a whole 2x2x4 slice. The times are simulated.
32 devices in a mesh: dp: 8 (over y, x, core), tensor: 4 (over z).
Axes of the slice: x: 2, y: 2, z: 4, core: 2. Of those that a mesh axis runs over, the one named last changes fastest.
Arguments:
- tokens: bfloat16 [8192, 2048], P(('dp', 'tensor')), may hold values from -6 to 6
- w_qkv: float32 [3, 2048, 2048], P(None, 'dp', 'tensor'), may hold values from -0.125 to 0.125
- w_out: float32 [2048, 2048], P('tensor', 'dp'), may hold values from -0.5 to 0.5
- w_up: float32 [2048, 8192], P('dp', 'tensor'), may hold values from -0.125 to 0.125
- w_down: float32 [8192, 2048], P('tensor', 'dp'), may hold values from -0.0625 to 0.0625
- norm_gains: float32 [2, 2048], P(None, 'dp'), may hold values from 0.25 to 1.75
- norm_biases: float32 [2, 2048], P(None, 'dp'), may hold values from -1.75 to 1.75
- lengths: int32 [8], P('dp'), may hold values from 256 to 1024, as said below
- cotangent: bfloat16 [8192, 2048], P(('dp', 'tensor')), may hold values from -6 to 6
Outputs:
- output: bfloat16 [8192, 2048], P(('dp', 'tensor'))
- input_grad: bfloat16 [8192, 2048], P(('dp', 'tensor'))
- grad_qkv: float32 [3, 2048, 2048], P(None, 'dp', 'tensor')
- grad_out: float32 [2048, 2048], P('tensor', 'dp')
- grad_up: float32 [2048, 8192], P('dp', 'tensor')
- grad_down: float32 [8192, 2048], P('tensor', 'dp')
- gain_grads: float32 [2, 2048], P(None, ('dp', 'tensor'))
- bias_grads: float32 [2, 2048], P(None, ('dp', 'tensor'))
Inputs may be any that keep to these rules, and one draw needn't show every extreme that they name: `lengths`: one sequence has exactly 1024 valid slots and one exactly 256.
All inputs are finite; a program needn't handle non-finite values.
Results may differ from a plain program's by a relative error of at most 0.019.
Values may be sent and summed in bfloat16 or wider, within the bound.
A program may use at most 192 MiB of HBM per device.

v0:
```python
import math

import jax
import jax.numpy as jnp
from jax import lax
from jax.sharding import PartitionSpec as P

HEAD_DIM = 64
SEQ_LEN = 1024
BLOCK = 512


EPSILON = 1e-05
MASKED = -1e30
INV_ROOT_TAU = 0.3989422804014327
ROOT_HALF = 0.7071067811865476


def dot_plain(left, right):
    return jnp.dot(left, right, preferred_element_type=jnp.float32)


def dot_rows(left, right):
    return lax.dot_general(
        left, right, (((0,), (0,)), ((), ())), preferred_element_type=jnp.float32
    )


def dot_cols(left, right):
    return lax.dot_general(
        left, right, (((1,), (1,)), ((), ())), preferred_element_type=jnp.float32
    )


def normalize(values):
    center = jnp.mean(values, axis=-1, keepdims=True)
    offset = values - center
    spread = jnp.mean(offset * offset, axis=-1, keepdims=True)
    inv_std = lax.rsqrt(spread + EPSILON)
    return (offset * inv_std, inv_std)


def norm_back(grads, normed, inv_std, gain):
    scaled = grads * gain
    return inv_std * (
        scaled
        - jnp.mean(scaled, axis=-1, keepdims=True)
        - normed * jnp.mean(scaled * normed, axis=-1, keepdims=True)
    )


def block_scores(query_blk, key_prefix, blk_start, slopes, lengths):
    count = query_blk.shape[1]
    width = key_prefix.shape[1]
    scale = 1.0 / math.sqrt(query_blk.shape[3])
    scores = (
        jnp.einsum("sqhd,skhd->shqk", query_blk, key_prefix, preferred_element_type=jnp.float32)
        * scale
    )
    row_pos = blk_start + jnp.arange(count, dtype=jnp.int32)
    key_pos = jnp.arange(width, dtype=jnp.int32)
    distance = (row_pos[:, None] - key_pos[None, :]).astype(jnp.float32)
    scores = scores - slopes[None, :, None, None] * distance[None, None]
    causal = key_pos[None, :] <= row_pos[:, None]
    allowed = causal[None] & (key_pos[None, None, :] < lengths[:, None, None])
    return jnp.where(allowed[:, None], scores, MASKED)


def attention_forward(queries, keys_all, values_all, slopes, lengths):
    outputs = []
    row_tops = []
    row_totals = []
    for blk_index in range(SEQ_LEN // BLOCK):
        blk_start = blk_index * BLOCK
        blk_end = blk_start + BLOCK
        scores = block_scores(
            queries[:, blk_start:blk_end], keys_all[:, :blk_end], blk_start, slopes, lengths
        )
        row_top = jnp.max(scores, axis=-1, keepdims=True)
        weights = jnp.exp(scores - row_top)
        row_total = jnp.sum(weights, axis=-1, keepdims=True)
        row_probs = (weights / row_total).astype(jnp.bfloat16)
        outputs.append(
            jnp.einsum(
                "shqk,skhd->sqhd",
                row_probs,
                values_all[:, :blk_end],
                preferred_element_type=jnp.float32,
            )
        )
        row_tops.append(row_top)
        row_totals.append(row_total)
    return (jnp.concatenate(outputs, axis=1), row_tops, row_totals)


def attention_backward(
    queries, keys_all, values_all, d_attn, slopes, lengths, row_tops, row_totals
):
    scale = 1.0 / math.sqrt(queries.shape[3])
    query_grads = []
    key_grads = jnp.zeros(keys_all.shape, jnp.float32)
    value_grads = jnp.zeros(values_all.shape, jnp.float32)
    for blk_index in range(SEQ_LEN // BLOCK):
        blk_start = blk_index * BLOCK
        blk_end = blk_start + BLOCK
        query_blk = queries[:, blk_start:blk_end]
        grad_blk = d_attn[:, blk_start:blk_end]
        scores = block_scores(query_blk, keys_all[:, :blk_end], blk_start, slopes, lengths)
        row_probs = jnp.exp(scores - row_tops[blk_index]) / row_totals[blk_index]
        d_probs = jnp.einsum(
            "sqhd,skhd->shqk", grad_blk, values_all[:, :blk_end], preferred_element_type=jnp.float32
        )
        weighted = jnp.sum(row_probs * d_probs, axis=-1, keepdims=True)
        d_scores = (row_probs * (d_probs - weighted)).astype(jnp.bfloat16)
        query_grads.append(
            jnp.einsum(
                "shqk,skhd->sqhd",
                d_scores,
                keys_all[:, :blk_end],
                preferred_element_type=jnp.float32,
            )
            * scale
        )
        key_grads = key_grads.at[:, :blk_end].add(
            jnp.einsum("shqk,sqhd->skhd", d_scores, query_blk, preferred_element_type=jnp.float32)
            * scale
        )
        value_grads = value_grads.at[:, :blk_end].add(
            jnp.einsum(
                "shqk,sqhd->skhd",
                row_probs.astype(jnp.bfloat16),
                grad_blk,
                preferred_element_type=jnp.float32,
            )
        )
    return (jnp.concatenate(query_grads, axis=1), key_grads, value_grads)


def per_device(tokens, w_qkv, w_out, w_up, w_down, norm_gains, norm_biases, lengths, cotangent):
    bf16 = jnp.bfloat16
    rows_dev = tokens.shape[0]
    seqs = lengths.shape[0]
    group_rows = seqs * SEQ_LEN
    fetched = (
        lax.all_gather(w_qkv.astype(bf16), "dp", axis=1, tiled=True),
        lax.all_gather(w_out.astype(bf16), "dp", axis=1, tiled=True),
        lax.all_gather(w_up.astype(bf16), "dp", axis=0, tiled=True),
        lax.all_gather(w_down.astype(bf16), "dp", axis=1, tiled=True),
        lax.all_gather(norm_gains.astype(bf16), "dp", axis=1, tiled=True),
        lax.all_gather(norm_biases.astype(bf16), "dp", axis=1, tiled=True),
    )
    qkv_all, out_all, up_all, down_all, gains_all, shifts_all = fetched
    gains = gains_all.astype(jnp.float32)
    shifts = shifts_all.astype(jnp.float32)
    heads_local = qkv_all.shape[2] // HEAD_DIM
    head_ids = (
        lax.axis_index("tensor") * heads_local + jnp.arange(heads_local, dtype=jnp.int32)
    ).astype(jnp.float32)
    heads_total = heads_local * lax.axis_size("tensor")
    slopes = jnp.exp2(-8.0 * (head_ids + 1.0) / heads_total)
    own_start = lax.axis_index("tensor") * rows_dev
    group_pos = own_start + jnp.arange(rows_dev, dtype=jnp.int32)
    seq_of_row = group_pos // SEQ_LEN
    slot_pos = group_pos % SEQ_LEN
    seq_match = seq_of_row[:, None] == jnp.arange(seqs, dtype=jnp.int32)[None, :]
    row_length = jnp.sum(jnp.where(seq_match, lengths[None, :], 0), axis=1)
    live_rows = (slot_pos < row_length)[:, None]
    inputs = tokens.astype(jnp.float32)
    hat_one, inv_one = normalize(inputs)
    normed_one = (hat_one * gains[0] + shifts[0]).astype(bf16)
    normed_one_all = lax.all_gather(normed_one, "tensor", axis=0, tiled=True)
    queries = dot_plain(normed_one_all, qkv_all[0]).astype(bf16)
    keys_all = dot_plain(normed_one_all, qkv_all[1]).astype(bf16)
    values_all = dot_plain(normed_one_all, qkv_all[2]).astype(bf16)
    head_shape = (seqs, SEQ_LEN, heads_local, HEAD_DIM)
    attn_f, row_tops, row_totals = attention_forward(
        queries.reshape(head_shape),
        keys_all.reshape(head_shape),
        values_all.reshape(head_shape),
        slopes,
        lengths,
    )
    attn_low = attn_f.reshape(group_rows, heads_local * HEAD_DIM).astype(bf16)
    attn_branch = lax.psum_scatter(
        dot_plain(attn_low, out_all).astype(jnp.bfloat16), "tensor", scatter_dimension=0, tiled=True
    ).astype(jnp.float32)
    after_attn = inputs + attn_branch
    hat_two, inv_two = normalize(after_attn)
    normed_two = (hat_two * gains[1] + shifts[1]).astype(bf16)
    normed_two_all = lax.all_gather(normed_two, "tensor", axis=0, tiled=True)
    pre_act = dot_plain(normed_two_all, up_all)
    activated = jax.nn.gelu(pre_act, approximate=False).astype(bf16)
    mlp_branch = lax.psum_scatter(
        dot_plain(activated, down_all).astype(jnp.bfloat16),
        "tensor",
        scatter_dimension=0,
        tiled=True,
    ).astype(jnp.float32)
    output = jnp.where(live_rows, after_attn + mlp_branch, 0.0).astype(bf16)
    again = (
        lax.all_gather(w_qkv.astype(bf16), "dp", axis=1, tiled=True),
        lax.all_gather(w_out.astype(bf16), "dp", axis=1, tiled=True),
        lax.all_gather(w_up.astype(bf16), "dp", axis=0, tiled=True),
        lax.all_gather(w_down.astype(bf16), "dp", axis=1, tiled=True),
    )
    qkv_back, out_back, up_back, down_back = again
    masked_cot = jnp.where(live_rows, cotangent, jnp.zeros_like(cotangent))
    masked_cot_all = lax.all_gather(masked_cot, "tensor", axis=0, tiled=True)
    d_act = dot_cols(masked_cot_all, down_back)
    grad_down = dot_rows(activated, masked_cot_all)
    gelu_slope = (
        0.5 * (1.0 + lax.erf(pre_act * ROOT_HALF))
        + pre_act * jnp.exp(-0.5 * pre_act * pre_act) * INV_ROOT_TAU
    )
    d_up = (d_act * gelu_slope).astype(bf16)
    grad_up = dot_rows(normed_two_all, d_up)
    d_norm_two = lax.psum_scatter(
        dot_cols(d_up, up_back).astype(jnp.bfloat16), "tensor", scatter_dimension=0, tiled=True
    ).astype(jnp.float32)
    gain_two = jnp.sum(d_norm_two * hat_two, axis=0)
    shift_two = jnp.sum(d_norm_two, axis=0)
    d_after = masked_cot.astype(jnp.float32) + norm_back(d_norm_two, hat_two, inv_two, gains[1])
    d_branch = d_after.astype(bf16)
    d_branch_all = lax.all_gather(d_branch, "tensor", axis=0, tiled=True)
    d_attn = dot_cols(d_branch_all, out_back).astype(bf16)
    grad_out = dot_rows(attn_low, d_branch_all)
    query_grads, key_grads, value_grads = attention_backward(
        queries.reshape(head_shape),
        keys_all.reshape(head_shape),
        values_all.reshape(head_shape),
        d_attn.reshape(head_shape),
        slopes,
        lengths,
        row_tops,
        row_totals,
    )
    flat_shape = (group_rows, heads_local * HEAD_DIM)
    d_queries = query_grads.reshape(flat_shape).astype(bf16)
    d_keys = key_grads.reshape(flat_shape).astype(bf16)
    d_values = value_grads.reshape(flat_shape).astype(bf16)
    grad_qkv = jnp.stack(
        [
            dot_rows(normed_one_all, d_queries),
            dot_rows(normed_one_all, d_keys),
            dot_rows(normed_one_all, d_values),
        ]
    )
    qkv_shard, out_shard, up_shard, down_shard = (
        lax.psum_scatter(
            grad_qkv.astype(jnp.bfloat16), "dp", scatter_dimension=1, tiled=True
        ).astype(jnp.float32),
        lax.psum_scatter(
            grad_out.astype(jnp.bfloat16), "dp", scatter_dimension=1, tiled=True
        ).astype(jnp.float32),
        lax.psum_scatter(
            grad_up.astype(jnp.bfloat16), "dp", scatter_dimension=0, tiled=True
        ).astype(jnp.float32),
        lax.psum_scatter(
            grad_down.astype(jnp.bfloat16), "dp", scatter_dimension=1, tiled=True
        ).astype(jnp.float32),
    )
    part_q = dot_cols(d_queries, qkv_back[0])
    part_k = dot_cols(d_keys, qkv_back[1])
    part_v = dot_cols(d_values, qkv_back[2])
    d_norm_one = lax.psum_scatter(
        (part_q + part_k + part_v).astype(jnp.bfloat16), "tensor", scatter_dimension=0, tiled=True
    ).astype(jnp.float32)
    gain_one = jnp.sum(d_norm_one * hat_one, axis=0)
    shift_one = jnp.sum(d_norm_one, axis=0)
    input_grad = (d_after + norm_back(d_norm_one, hat_one, inv_one, gains[0])).astype(bf16)
    gain_local = jnp.stack([gain_one, gain_two])
    shift_local = jnp.stack([shift_one, shift_two])
    gain_grads, bias_grads = (
        lax.psum_scatter(gain_local, ("dp", "tensor"), scatter_dimension=1, tiled=True),
        lax.psum_scatter(shift_local, ("dp", "tensor"), scatter_dimension=1, tiled=True),
    )
    return (output, input_grad, qkv_shard, out_shard, up_shard, down_shard, gain_grads, bias_grads)


def solution(mesh):
    placed = (
        P(("dp", "tensor"), None),
        P(None, "dp", "tensor"),
        P("tensor", "dp"),
        P("dp", "tensor"),
        P("tensor", "dp"),
        P(None, "dp"),
        P(None, "dp"),
        P("dp"),
        P(("dp", "tensor"), None),
    )
    return jax.shard_map(
        per_device,
        mesh=mesh,
        in_specs=placed,
        out_specs=(
            P(("dp", "tensor"), None),
            P(("dp", "tensor"), None),
            P(None, "dp", "tensor"),
            P("tensor", "dp"),
            P("dp", "tensor"),
            P("tensor", "dp"),
            P(None, ("dp", "tensor")),
            P(None, ("dp", "tensor")),
        ),
        check_vma=False,
    )
```

profile of v0, /device:TPU:0, one launch (start us, length us, event | category | flops | bytes accessed | tf_op | source)
XLA Modules:
  0.0 1531.7 jit_solution(12505957222165873398)
XLA Ops:
  11.9 10.4 all_gather.35
  22.3 8.9 all_gather.34
  39.6 75.5 %all-gather.9.cloned.1.call-done = bf16[1024,2048]{1,0:T(8,128)(2,1)} async-done(((bf16[256,2048]{1,0:T(8,128)(2,1)}), bf16[1024,2048]{1,0:T(8,128)(2,1)}) %all-gather.9.cloned.1.call-update) | async-done | bytes 4194320 | tf_op jit(solution)/shard_map/all_gather | solution.py:171
  115.1 46.4 %all-gather.11.cloned.1.call-done = bf16[3,2048,512]{2,1,0:T(8,128)(2,1)} async-done(((bf16[3,256,512]{2,1,0:T(8,128)(2,1)}), bf16[3,2048,512]{2,1,0:T(8,128)(2,1)}) %all-gather.11.cloned.1.call-update) | async-done | bytes 6291472 | tf_op jit(solution)/shard_map/all_gather | solution.py:145
  174.2 11.8 fusion.118
  186.0 9.8 fusion.91
  195.8 8.5 fusion.119
  208.8 6.6 convolution_convert_fusion.4
  218.2 74.2 %reduce-scatter.15.cloned.1.call-done = bf16[256,2048]{1,0:T(8,128)(2,1)} async-done(((bf16[1024,2048]{1,0:T(8,128)(2,1)}), bf16[256,2048]{1,0:T(8,128)(2,1)}) %reduce-scatter.15.cloned.1.call-update) | async-done | bytes 1048592 | tf_op jit(solution)/shard_map/reduce_scatter | solution.py:184
  301.5 47.4 %all-gather.17.cloned.1.call-done = bf16[2048,2048]{1,0:T(8,128)(2,1)} async-done(((bf16[256,2048]{1,0:T(8,128)(2,1)}), bf16[2048,2048]{1,0:T(8,128)(2,1)}) %all-gather.17.cloned.1.call-update) | async-done | bytes 8388624 | tf_op jit(solution)/shard_map/all_gather | solution.py:147
  348.9 82.8 %all-gather.15.cloned.1.call-done = bf16[1024,2048]{1,0:T(8,128)(2,1)} async-done(((bf16[256,2048]{1,0:T(8,128)(2,1)}), bf16[1024,2048]{1,0:T(8,128)(2,1)}) %all-gather.15.cloned.1.call-update) | async-done | bytes 4194320 | tf_op jit(solution)/shard_map/all_gather | solution.py:190
  431.7 30.5 %fusion.5 = (bf16[1024,2048]{1,0:T(8,128)(2,1)}, f32[1024,2048]{1,0:T(8,128)}) fusion(bf16[1024,2048]{1,0:T(8,128)(2,1)} %all-gather.15.cloned.1.call-done, bf16[2048,2048]{1,0:T(8,128)(2,1)} %all-gather.17.cloned.1.call-done), kind=kOutput, calls=%fused_computation.11 | convolution fusion | flops 8726249472 | bytes 25165824 | tf_op jit(solution)/shard_map/dot_general | solution.py:20
  462.2 50.3 %all-gather.21.cloned.1.call-done = bf16[1024,2048]{1,0:T(8,128)(2,1)} async-done(((bf16[256,2048]{1,0:T(8,128)(2,1)}), bf16[1024,2048]{1,0:T(8,128)(2,1)}) %all-gather.21.cloned.1.call-update) | async-done | bytes 4194320 | tf_op jit(solution)/shard_map/all_gather | solution.py:208
  512.5 56.3 %all-gather.19.cloned.1.call-done = bf16[2048,2048]{1,0:T(8,128)(2,1)} async-done(((bf16[2048,256]{1,0:T(8,128)(2,1)}), bf16[2048,2048]{1,0:T(8,128)(2,1)}) %all-gather.19.cloned.1.call-update) | async-done | bytes 8388624 | tf_op jit(solution)/shard_map/all_gather | solution.py:148
  568.8 15.8 %fusion.11 = bf16[1024,2048]{1,0:T(8,128)(2,1)S(1)} fusion(f32[1024,2048]{1,0:T(8,128)} %get-tuple-element.95, bf16[1024,2048]{1,0:T(8,128)(2,1)} %all-gather.21.cloned.1.call-done, bf16[2048,2048]{1,0:T(8,128)(2,1)} %all-gather.19.cloned.1.call-done), kind=kOutput, calls=%fused_computation.17 | convolution fusion | flops 8610906112 | bytes 25165824 | tf_op jit(solution)/shard_map/dot_general | solution.py:30
  586.5 10.7 convolution_convert_fusion.2
  597.3 76.9 %reduce-scatter.19.cloned.1.call-done = bf16[256,2048]{1,0:T(8,128)(2,1)} async-done(((bf16[1024,2048]{1,0:T(8,128)(2,1)}), bf16[256,2048]{1,0:T(8,128)(2,1)}) %reduce-scatter.19.cloned.1.call-update) | async-done | bytes 1048592 | tf_op jit(solution)/shard_map/reduce_scatter | solution.py:217
  680.5 81.3 %all-gather.23.cloned.1.call-done = bf16[1024,2048]{1,0:T(8,128)(2,1)} async-done(((bf16[256,2048]{1,0:T(8,128)(2,1)}), bf16[1024,2048]{1,0:T(8,128)(2,1)}) %all-gather.23.cloned.1.call-update) | async-done | bytes 4194320 | tf_op jit(solution)/shard_map/all_gather | solution.py:224
  781.2 10.6 fusion.61
  791.8 13.6 multiply_reduce_fusion
  808.7 7.4 multiply_convert_fusion
  835.7 14.3 convolution_convert_fusion.1
  850.0 14.1 convolution_convert_fusion
  870.4 14.3 convolution_convert_fusion.3
  899.1 12.0 reduce-scatter.21.cloned.1.call-done
  922.1 64.3 %reduce-scatter.27.cloned.1.call-done = bf16[256,2048]{1,0:T(8,128)(2,1)} async-done(((bf16[2048,2048]{1,0:T(8,128)(2,1)}), bf16[256,2048]{1,0:T(8,128)(2,1)}) %reduce-scatter.27.cloned.1.call-update) | async-done | bytes 1048592 | tf_op jit(solution)/shard_map/reduce_scatter | solution.py:255
  989.2 72.0 %reduce-scatter.29.cloned.1.call-done = bf16[2048,256]{1,0:T(8,128)(2,1)} async-done(((bf16[2048,2048]{1,0:T(8,128)(2,1)}), bf16[2048,256]{1,0:T(8,128)(2,1)}) %reduce-scatter.29.cloned.1.call-update) | async-done | bytes 1048592 | tf_op jit(solution)/shard_map/reduce_scatter | solution.py:258
  1063.9 41.6 %reduce-scatter.25.cloned.1.call-done = bf16[512,256]{1,0:T(8,128)(2,1)} async-done(((bf16[512,2048]{1,0:T(8,128)(2,1)}), bf16[512,256]{1,0:T(8,128)(2,1)}) %reduce-scatter.25.cloned.1.call-update) | async-done | bytes 262160 | tf_op jit(solution)/shard_map/reduce_scatter | solution.py:252
  1107.3 77.2 %reduce-scatter.17.cloned.1.call-done = bf16[256,2048]{1,0:T(8,128)(2,1)} async-done(((bf16[1024,2048]{1,0:T(8,128)(2,1)}), bf16[256,2048]{1,0:T(8,128)(2,1)}) %reduce-scatter.17.cloned.1.call-update) | async-done | bytes 1048592 | tf_op jit(solution)/shard_map/reduce_scatter | solution.py:193
  1189.6 134.5 %reduce-scatter.33.cloned.1.call-done = f32[64,2]{1,0:T(8,128)} async-done(((f32[2048,2]{1,0:T(8,128)}), f32[64,2]{1,0:T(8,128)}) %reduce-scatter.33.cloned.1.call-update) | async-done | bytes 528
  1325.5 135.1 %reduce-scatter.31.cloned.1.call-done = f32[64,2]{1,0:T(8,128)} async-done(((f32[2048,2]{1,0:T(8,128)}), f32[64,2]{1,0:T(8,128)}) %reduce-scatter.31.cloned.1.call-update) | async-done | bytes 528
  1462.0 60.2 %reduce-scatter.23.cloned.1.call-done = bf16[3,256,512]{2,1,0:T(8,128)(2,1)} async-done(((bf16[3,2048,512]{2,1,0:T(8,128)(2,1)}), bf16[3,256,512]{2,1,0:T(8,128)(2,1)}) %reduce-scatter.23.cloned.1.call-update) | async-done | bytes 786448 | tf_op jit(solution)/shard_map/reduce_scatter | solution.py:249
  (220 shorter events, 140.7 us)
Async XLA Ops:
  7.2 107.9 %all-gather.9.cloned.1.call-start = ((), (), s32[]{:S(2)}) async-start(), calls=%async_computation.10 | async-start | bytes 5242880 | tf_op jit(solution)/shard_map/all_gather | solution.py:171
  31.2 645.9 %copy-start.20 = (f32[1,2048]{1,0:T(1,128)}, f32[1,2048]{1,0:T(1,128)S(1)}, u32[]{:S(2)}) copy-start(f32[1,2048]{1,0:T(1,128)S(1)} %get-tuple-element.83) | copy-start | bytes 24580
  33.9 127.5 %all-gather.11.cloned.1.call-start = ((), (), s32[]{:S(2)}) async-start(), calls=%async_computation.11 | async-start | bytes 7077888 | tf_op jit(solution)/shard_map/all_gather | solution.py:145
  35.0 173.8 %all-gather.13.cloned.1.call-start = ((), (), s32[]{:S(2)}) async-start(), calls=%async_computation.12 | async-start | bytes 2359296 | tf_op jit(solution)/shard_map/all_gather | solution.py:146
  35.9 256.5 %reduce-scatter.15.cloned.1.call-start = ((), (), s32[]{:S(2)}) async-start(), calls=%async_computation.13 | async-start | bytes 5242880 | tf_op jit(solution)/shard_map/reduce_scatter | solution.py:184
  37.7 158.1 %copy-start.48 = (f32[8]{0:T(128)}, f32[8]{0:T(128)S(1)}, u32[]{:S(2)}) copy-start(f32[8]{0:T(128)S(1)} %multiply_exponential_fusion) | copy-start | bytes 100
  38.1 147.9 %copy-start.9 = (f32[512,1024]{1,0:T(8,128)}, f32[512,1024]{1,0:T(8,128)S(1)}, u32[]{:S(2)}) copy-start(f32[512,1024]{1,0:T(8,128)S(1)} %subtract_convert_fusion) | copy-start | bytes 6291460
  215.4 133.5 %all-gather.17.cloned.1.call-start = ((), (), s32[]{:S(2)}) async-start(), calls=%async_computation.15 | async-start | bytes 9437184 | tf_op jit(solution)/shard_map/all_gather | solution.py:147
  218.1 213.5 %all-gather.15.cloned.1.call-start = ((), (), s32[]{:S(2)}) async-start(), calls=%async_computation.14 | async-start | bytes 5242880 | tf_op jit(solution)/shard_map/all_gather | solution.py:190
  294.0 383.1 %copy-start.24 = (f32[256]{0:T(256)}, f32[256]{0:T(256)S(1)}, u32[]{:S(2)}) copy-start(f32[256]{0:T(256)S(1)} %broadcast_multiply_fusion.4) | copy-start | bytes 3076
  295.8 381.4 %copy-start.30 = (f32[256]{0:T(256)}, f32[256]{0:T(256)S(1)}, u32[]{:S(2)}) copy-start(f32[256]{0:T(256)S(1)} %add_rsqrt_fusion) | copy-start | bytes 3076
  297.4 215.1 %all-gather.21.cloned.1.call-start = ((), (), s32[]{:S(2)}) async-start(), calls=%async_computation.18 | async-start | bytes 5242880 | tf_op jit(solution)/shard_map/all_gather | solution.py:208
  297.4 379.7 %copy-start.40 = (pred[256]{0:T(512)(128)(4,1)}, pred[256]{0:T(512)(128)(4,1)S(1)}, u32[]{:S(2)}) copy-start(pred[256]{0:T(512)(128)(4,1)S(1)} %fusion.109) | copy-start | bytes 772
  298.6 270.1 %all-gather.19.cloned.1.call-start = ((), (), s32[]{:S(2)}) async-start(), calls=%async_computation.16 | async-start | bytes 9437184 | tf_op jit(solution)/shard_map/all_gather | solution.py:148
  301.4 372.8 %reduce-scatter.19.cloned.1.call-start = ((), (), s32[]{:S(2)}) async-start(), calls=%async_computation.19 | async-start | bytes 5242880 | tf_op jit(solution)/shard_map/reduce_scatter | solution.py:217
  597.2 164.6 %all-gather.23.cloned.1.call-start = ((), (), s32[]{:S(2)}) async-start(), calls=%async_computation.20 | async-start | bytes 5242880 | tf_op jit(solution)/shard_map/all_gather | solution.py:224
  680.5 230.6 %reduce-scatter.21.cloned.1.call-start = ((), (), s32[]{:S(2)}) async-start(), calls=%async_computation.21 | async-start | bytes 5242880 | tf_op jit(solution)/shard_map/reduce_scatter | solution.py:265
  835.6 150.8 %reduce-scatter.27.cloned.1.call-start = ((), (), s32[]{:S(2)}) async-start(), calls=%async_computation.24 | async-start | bytes 9437184 | tf_op jit(solution)/shard_map/reduce_scatter | solution.py:255
  850.0 211.2 %reduce-scatter.29.cloned.1.call-start = ((), (), s32[]{:S(2)}) async-start(), calls=%async_computation.25 | async-start | bytes 9437184 | tf_op jit(solution)/shard_map/reduce_scatter | solution.py:258
  864.1 241.4 %reduce-scatter.25.cloned.1.call-start = ((), (), s32[]{:S(2)}) async-start(), calls=%async_computation.23 | async-start | bytes 2359296 | tf_op jit(solution)/shard_map/reduce_scatter | solution.py:252
  870.4 314.1 %reduce-scatter.17.cloned.1.call-start = ((), (), s32[]{:S(2)}) async-start(), calls=%async_computation.17 | async-start | bytes 5242880 | tf_op jit(solution)/shard_map/reduce_scatter | solution.py:193
  884.7 439.4 %reduce-scatter.33.cloned.1.call-start = ((), (), s32[]{:S(2)}) async-start(), calls=%async_computation.27 | async-start | bytes 1081344
  914.8 545.8 %reduce-scatter.31.cloned.1.call-start = ((), (), s32[]{:S(2)}) async-start(), calls=%async_computation.26 | async-start | bytes 1081344
  916.4 605.8 %reduce-scatter.23.cloned.1.call-start = ((), (), s32[]{:S(2)}) async-start(), calls=%async_computation.22 | async-start | bytes 7077888 | tf_op jit(solution)/shard_map/reduce_scatter | solution.py:249
  922.0 262.4 %copy-start.3 = (bf16[256,2048]{1,0:T(8,128)(2,1)S(1)}, bf16[256,2048]{1,0:T(8,128)(2,1)}, u32[]{:S(2)}) copy-start(bf16[256,2048]{1,0:T(8,128)(2,1)} %reduce-scatter.15.cloned.1.call-done) | copy-start | bytes 3145732
  922.0 262.4 %copy-start.5 = (bf16[256,2048]{1,0:T(8,128)(2,1)S(1)}, bf16[256,2048]{1,0:T(8,128)(2,1)}, u32[]{:S(2)}) copy-start(bf16[256,2048]{1,0:T(8,128)(2,1)} %param.29) | copy-start | bytes 3145732
  922.0 262.4 %copy-start.21 = (f32[1,2048]{1,0:T(1,128)S(1)}, f32[1,2048]{1,0:T(1,128)}, u32[]{:S(2)}) copy-start(f32[1,2048]{1,0:T(1,128)} %copy-done.20) | copy-start | bytes 24580
  922.0 262.4 %copy-start.25 = (f32[256]{0:T(256)S(1)}, f32[256]{0:T(256)}, u32[]{:S(2)}) copy-start(f32[256]{0:T(256)} %copy-done.24) | copy-start | bytes 3076
  922.0 262.4 %copy-start.31 = (f32[256]{0:T(256)S(1)}, f32[256]{0:T(256)}, u32[]{:S(2)}) copy-start(f32[256]{0:T(256)} %copy-done.30) | copy-start | bytes 3076
  922.1 262.4 %copy-start.37 = (f32[256]{0:T(256)S(1)}, f32[256]{0:T(256)}, u32[]{:S(2)}) copy-start(f32[256]{0:T(256)} %copy-done.36) | copy-start | bytes 3076
  922.1 262.4 %copy-start.39 = (f32[256]{0:T(256)S(1)}, f32[256]{0:T(256)}, u32[]{:S(2)}) copy-start(f32[256]{0:T(256)} %copy-done.38) | copy-start | bytes 3076
  922.1 262.4 %copy-start.41 = (pred[256]{0:T(512)(128)(4,1)S(1)}, pred[256]{0:T(512)(128)(4,1)}, u32[]{:S(2)}) copy-start(pred[256]{0:T(512)(128)(4,1)} %copy-done.40) | copy-start | bytes 772
  (43 other events, 774.1 us)
Sparse Core Ops, SparseCore 0:
  34.1 80.9 all-gather.8
  117.6 43.8 all-gather.10
  163.4 28.0 all-gather.12
  215.5 76.7 reduce-scatter.14
  294.1 54.7 all-gather.16
  350.9 80.7 all-gather.14
  433.2 79.2 all-gather.20
  514.4 54.3 all-gather.18
  597.3 76.8 reduce-scatter.18
  680.6 81.2 all-gather.22
  835.7 75.2 reduce-scatter.20
  914.4 72.0 reduce-scatter.26
  989.9 71.2 reduce-scatter.28
  1064.3 41.1 reduce-scatter.24
  1107.6 76.7 reduce-scatter.16
  1186.5 137.5 reduce-scatter.32
  1326.8 133.7 reduce-scatter.30
  1463.8 58.2 reduce-scatter.22
where the time goes:
time: 1540 us; the launch traced here: 1530 us
  waiting for transfers between devices  1190 us (77%)
  matrix products  233 us (15%)
  other arithmetic  60.9 us (4%)
  blocking collectives  19.3 us (1%)
  between operations  15.9 us (1%)
    unnamed x20, waiting for transfers between devices  270 us
    all_gather x1, waiting for transfers between devices, per_device(): normed_two_all = lax.all_gather(normed_two, 'tensor', axis=0, tiled=True)  82.8 us
    all_gather x1, waiting for transfers between devices, per_device(): d_branch_all = lax.all_gather(d_branch, 'tensor', axis=0, tiled=True)  81.3 us
    reduce_scatter x1, waiting for transfers between devices, per_device(): lax.psum_scatter(dot_plain(activated, down_all).astype(jnp.bfloat16), 'te...  77.2 us
    reduce_scatter x1, waiting for transfers between devices, per_device(): lax.psum_scatter(dot_cols(d_up, up_back).astype(jnp.bfloat16), 'tensor',...  76.9 us
    all_gather x1, waiting for transfers between devices, per_device(): normed_one_all = lax.all_gather(normed_one, 'tensor', axis=0, tiled=True)  75.5 us
    reduce_scatter x1, waiting for transfers between devices, per_device(): lax.psum_scatter(dot_plain(attn_low, out_all).astype(jnp.bfloat16), 'tens...  74.2 us
    reduce_scatter x1, waiting for transfers between devices, per_device(): lax.psum_scatter(grad_down.astype(jnp.bfloat16), 'dp', scatter_dimension=...  72 us
  transfers between devices with their start and end apart: 18, of which 17 were waited for; matrix products, arithmetic and copies ran while one was open for 12% of the time, Pallas kernels for 0%

commit v1 on v0

v1 whole, which is shorter than its diff:
```python
import functools

import jax
import jax.numpy as jnp
from jax import lax
from jax.experimental import pallas as pl
from jax.experimental.pallas import tpu as pltpu
from jax.sharding import PartitionSpec as P

HEAD_DIM = 64
LANES = 128
TILE = 256
PARTS = 4
VMEM_BYTES = 60 * 1024 * 1024

EPSILON = 1e-05
MASKED = -1e30
INV_ROOT_TAU = 0.3989422804014327
ROOT_HALF = 0.7071067811865476

MESH = pl.DeviceIdType.MESH
ANY = pl.BlockSpec(memory_space=pl.ANY)
F32 = jnp.float32
BF16 = jnp.bfloat16


def dot_nn(left, right):
    return lax.dot_general(left, right, (((1,), (0,)), ((), ())), preferred_element_type=F32)


def dot_nt(left, right):
    return lax.dot_general(left, right, (((1,), (1,)), ((), ())), preferred_element_type=F32)


def dot_tn(left, right):
    return lax.dot_general(left, right, (((0,), (0,)), ((), ())), preferred_element_type=F32)


def normalize(values):
    center = jnp.mean(values, axis=-1, keepdims=True)
    offset = values - center
    spread = jnp.mean(offset * offset, axis=-1, keepdims=True)
    inv_std = lax.rsqrt(spread + EPSILON)
    return (offset * inv_std, inv_std)


def norm_back(grads, normed, inv_std, gain):
    scaled = grads * gain
    return inv_std * (
        scaled
        - jnp.mean(scaled, axis=-1, keepdims=True)
        - normed * jnp.mean(scaled * normed, axis=-1, keepdims=True)
    )


def block_at(index, size):
    return pl.ds(pl.multiple_of(index * size, size), size)


def line_enter(p, n):
    barrier = pltpu.get_barrier_semaphore()

    @pl.when(p > 0)
    def _():
        pl.semaphore_signal(barrier, inc=1, device_id={"tensor": p - 1}, device_id_type=MESH)

    @pl.when(p < n - 1)
    def _():
        pl.semaphore_signal(barrier, inc=1, device_id={"tensor": p + 1}, device_id_type=MESH)

    pl.semaphore_wait(barrier, jnp.where(p > 0, 1, 0) + jnp.where(p < n - 1, 1, 0))


class Line:
    def __init__(self, n, rows):
        self.n = n
        self.p = lax.axis_index("tensor")
        self.rows = rows
        self.piece = rows // PARTS
        self.right = lax.rem(self.p + 1, n)
        self.left = lax.rem(self.p + n - 1, n)

    def slot(self, ref, j, c):
        start = pl.multiple_of(j * self.rows + c * self.piece, self.piece)
        return ref.at[pl.ds(start, self.piece)]

    def shard(self, ref, j):
        return ref.at[block_at(j, self.rows)]


class Gather:
    def __init__(self, line, buf, right_sem, left_sem, recv_sem):
        self.line, self.buf = line, buf
        self.right_sem, self.left_sem, self.recv_sem = right_sem, left_sem, recv_sem

    def copy(self, j, c, rightward):
        line = self.line
        slot = line.slot(self.buf, j, c)
        i = j * PARTS + c
        return pltpu.make_async_remote_copy(
            src_ref=slot,
            dst_ref=slot,
            send_sem=(self.right_sem if rightward else self.left_sem).at[i],
            recv_sem=self.recv_sem.at[i],
            device_id={"tensor": line.right if rightward else line.left},
            device_id_type=MESH,
        )

    def begin(self):
        p, n = self.line.p, self.line.n
        for c in range(PARTS):

            @pl.when(p < n - 1)
            def _():
                self.copy(p, c, True).start()

            @pl.when(p > 0)
            def _():
                self.copy(p, c, False).start()

    def step(self, s, c):
        p, n = self.line.p, self.line.n

        @pl.when(p - s >= 0)
        def _():
            copy = self.copy(p - s, c, True)
            copy.wait_recv()

            @pl.when(p < n - 1)
            def _():
                copy.start()

        @pl.when(p + s < n)
        def _():
            copy = self.copy(p + s, c, False)
            copy.wait_recv()

            @pl.when(p > 0)
            def _():
                copy.start()

    def end(self):
        p, n = self.line.p, self.line.n

        @pl.loop(0, n)
        def _(j):
            for c in range(PARTS):

                @pl.when((j <= p) & (p < n - 1))
                def _():
                    self.copy(j, c, True).wait_send()

                @pl.when((j >= p) & (p > 0))
                def _():
                    self.copy(j, c, False).wait_send()


class Scatter:
    def __init__(self, line, part, from_left, from_right, right_sem, left_sem, lrecv_sem, rrecv_sem):
        self.line, self.part, self.from_left, self.from_right = line, part, from_left, from_right
        self.right_sem, self.left_sem = right_sem, left_sem
        self.lrecv_sem, self.rrecv_sem = lrecv_sem, rrecv_sem

    def copy(self, j, c, rightward):
        line = self.line
        i = j * PARTS + c
        return pltpu.make_async_remote_copy(
            src_ref=line.slot(self.part, j, c),
            dst_ref=line.slot(self.from_left if rightward else self.from_right, j, c),
            send_sem=(self.right_sem if rightward else self.left_sem).at[i],
            recv_sem=(self.lrecv_sem if rightward else self.rrecv_sem).at[i],
            device_id={"tensor": line.right if rightward else line.left},
            device_id_type=MESH,
        )

    def add(self, j, c, ref):
        part = self.line.slot(self.part, j, c)
        total = part[...].astype(F32) + self.line.slot(ref, j, c)[...].astype(F32)
        part[...] = total.astype(BF16)

    def send_right(self, j, c):
        p, n = self.line.p, self.line.n

        @pl.when((j > p) & (j < n))
        def _():
            copy = self.copy(j, c, True)

            @pl.when(p > 0)
            def _():
                copy.wait_recv()
                self.add(j, c, self.from_left)

            copy.start()

    def send_left(self, j, c):
        p, n = self.line.p, self.line.n

        @pl.when((j < p) & (j >= 0))
        def _():
            copy = self.copy(j, c, False)

            @pl.when(p < n - 1)
            def _():
                copy.wait_recv()
                self.add(j, c, self.from_right)

            copy.start()

    def finish(self, out):
        p, n = self.line.p, self.line.n
        piece = self.line.piece
        for c in range(PARTS):
            mine = out.at[pl.ds(c * piece, piece)]
            mine[...] = self.line.slot(self.part, p, c)[...].astype(F32)

            @pl.when(p > 0)
            def _():
                self.copy(p, c, True).wait_recv()
                mine[...] += self.line.slot(self.from_left, p, c)[...].astype(F32)

            @pl.when(p < n - 1)
            def _():
                self.copy(p, c, False).wait_recv()
                mine[...] += self.line.slot(self.from_right, p, c)[...].astype(F32)

    def end(self):
        p, n = self.line.p, self.line.n

        @pl.loop(0, n)
        def _(j):
            for c in range(PARTS):

                @pl.when(j > p)
                def _():
                    self.copy(j, c, True).wait_send()

                @pl.when(j < p)
                def _():
                    self.copy(j, c, False).wait_send()


def line_sems(n):
    return pltpu.SemaphoreType.DMA((n * PARTS,))


def remote_call(body, name, collective_id, outs, scratch, micros, *args):
    return pl.pallas_call(
        body,
        name=name,
        out_shape=outs,
        in_specs=[ANY] * len(args),
        out_specs=jax.tree.map(lambda _: ANY, outs),
        scratch_shapes=scratch,
        cost_estimate=pl.CostEstimate(
            flops=int(micros * 1e-6 * 1.15e15), bytes_accessed=1 << 20, transcendentals=0
        ),
        compiler_params=pltpu.CompilerParams(
            collective_id=collective_id, has_side_effects=True, vmem_limit_bytes=VMEM_BYTES
        ),
    )(*args)


def project_kernel(
    n, rows, h_ref, w_ref, qkv_ref, all_ref, buf, w_v, o_v, right_sem, left_sem, recv_sem, load_sem, q_sem, h_sem
):
    line = Line(n, rows)
    p = line.p
    width = w_v.shape[2]
    load_w = pltpu.make_async_copy(w_ref, w_v, load_sem.at[0])
    load_h = pltpu.make_async_copy(h_ref, line.shard(buf, p), load_sem.at[1])
    load_h.start()
    load_w.start()
    line_enter(p, n)
    load_h.wait()
    gather = Gather(line, buf, right_sem, left_sem, recv_sem)
    gather.begin()

    def stores(j):
        at = block_at(j, rows)
        return (
            pltpu.make_async_copy(o_v.at[:, at], qkv_ref.at[:, at], q_sem.at[j]),
            pltpu.make_async_copy(buf.at[at], all_ref.at[at], h_sem.at[j]),
        )

    def compute(j):
        at = block_at(j, rows)
        for i in range(3):

            @pl.loop(0, width // TILE)
            def _(t):
                cols = block_at(t, TILE)
                o_v[i, at, cols] = dot_nn(buf[at, :], w_v[i, :, cols]).astype(BF16)

        for copy in stores(j):
            copy.start()

    load_w.wait()
    compute(p)

    @pl.loop(1, n)
    def _(s):
        for c in range(PARTS):
            gather.step(s, c)

        @pl.when(p - s >= 0)
        def _():
            compute(p - s)

        @pl.when(p + s < n)
        def _():
            compute(p + s)

    gather.end()

    @pl.loop(0, n)
    def _(j):
        for copy in stores(j):
            copy.wait()


def project(normed, weights, n):
    rows, model = normed.shape
    width = weights.shape[2]
    group = n * rows
    return remote_call(
        functools.partial(project_kernel, n, rows),
        "project",
        1,
        (jax.ShapeDtypeStruct((3, group, width), BF16), jax.ShapeDtypeStruct((group, model), BF16)),
        [
            pltpu.VMEM((group, model), BF16),
            pltpu.VMEM(weights.shape, BF16),
            pltpu.VMEM((3, group, width), BF16),
            line_sems(n),
            line_sems(n),
            line_sems(n),
            pltpu.SemaphoreType.DMA((2,)),
            pltpu.SemaphoreType.DMA((n,)),
            pltpu.SemaphoreType.DMA((n,)),
        ],
        78,
        normed,
        weights,
    )


def branch_kernel(
    n, rows, attn_ref, w_ref, g_ref, out_ref, all_ref,
    a_v, w_v, buf, part, from_left, from_right, out_v,
    gr_sem, gl_sem, grecv_sem, sr_sem, sl_sem, lrecv_sem, rrecv_sem, load_sem, store_sem,
):
    line = Line(n, rows)
    p = line.p
    model = w_v.shape[1]
    loads = (
        pltpu.make_async_copy(g_ref, line.shard(buf, p), load_sem.at[0]),
        pltpu.make_async_copy(attn_ref, a_v, load_sem.at[1]),
        pltpu.make_async_copy(w_ref, w_v, load_sem.at[2]),
    )
    for copy in loads:
        copy.start()
    line_enter(p, n)
    for copy in loads:
        copy.wait()
    gather = Gather(line, buf, gr_sem, gl_sem, grecv_sem)
    scatter = Scatter(line, part, from_left, from_right, sr_sem, sl_sem, lrecv_sem, rrecv_sem)
    gather.begin()

    def compute(j):
        at = block_at(j, rows)

        @pl.loop(0, model // TILE)
        def _(t):
            cols = block_at(t, TILE)
            part[at, cols] = dot_nn(a_v[at, :], w_v[:, cols]).astype(BF16)

    @pl.loop(0, n)
    def _(s):
        right, left = n - 1 - s, s

        @pl.when(right > p)
        def _():
            compute(right)

        @pl.when(left < p)
        def _():
            compute(left)

        for c in range(PARTS):
            scatter.send_right(right, c)
            scatter.send_left(left, c)

            @pl.when(s + 1 < n)
            def _():
                gather.step(s + 1, c)

    compute(p)
    scatter.finish(out_v)
    stores = (
        pltpu.make_async_copy(out_v, out_ref, store_sem.at[0]),
        pltpu.make_async_copy(buf, all_ref, store_sem.at[1]),
    )
    for copy in stores:
        copy.start()
    scatter.end()
    gather.end()
    for copy in stores:
        copy.wait()


def branch(attn, w_out, cot, n):
    rows, model = cot.shape
    group = n * rows
    full = pltpu.VMEM((group, model), BF16)
    return remote_call(
        functools.partial(branch_kernel, n, rows),
        "branch",
        2,
        (jax.ShapeDtypeStruct((rows, model), F32), jax.ShapeDtypeStruct((group, model), BF16)),
        [
            pltpu.VMEM(attn.shape, BF16),
            pltpu.VMEM(w_out.shape, BF16),
            full, full, full, full,
            pltpu.VMEM((rows, model), F32),
        ]
        + [line_sems(n)] * 7
        + [pltpu.SemaphoreType.DMA((3,)), pltpu.SemaphoreType.DMA((2,))],
        100,
        attn,
        w_out,
        cot,
    )


def feed_kernel(
    n, rows, h_ref, g_ref, up_ref, down_ref, all_ref, act_ref, dup_ref, mlp_ref, dh_ref,
    buf, up_v, down_v, g_v, act_v, dup_v, mlp_v, part, from_left, from_right, out_v,
    gr_sem, gl_sem, grecv_sem, sr_sem, sl_sem, lrecv_sem, rrecv_sem, load_sem, store_sem,
):
    line = Line(n, rows)
    p = line.p
    model, hidden = up_v.shape
    load_h = pltpu.make_async_copy(h_ref, line.shard(buf, p), load_sem.at[0])
    loads = (
        pltpu.make_async_copy(up_ref, up_v, load_sem.at[1]),
        pltpu.make_async_copy(g_ref, g_v, load_sem.at[2]),
        pltpu.make_async_copy(down_ref, down_v, load_sem.at[3]),
    )
    load_h.start()
    for copy in loads:
        copy.start()
    line_enter(p, n)
    load_h.wait()
    gather = Gather(line, buf, gr_sem, gl_sem, grecv_sem)
    scatter = Scatter(line, part, from_left, from_right, sr_sem, sl_sem, lrecv_sem, rrecv_sem)
    gather.begin()
    for copy in loads:
        copy.wait()

    def stores(j):
        at = block_at(j, rows)
        return (
            pltpu.make_async_copy(buf.at[at], all_ref.at[at], store_sem.at[0, j]),
            pltpu.make_async_copy(act_v.at[at], act_ref.at[at], store_sem.at[1, j]),
            pltpu.make_async_copy(dup_v.at[at], dup_ref.at[at], store_sem.at[2, j]),
            pltpu.make_async_copy(mlp_v.at[at], mlp_ref.at[at], store_sem.at[3, j]),
        )

    def compute(j):
        at = block_at(j, rows)

        @pl.loop(0, hidden // TILE)
        def _(t):
            cols = block_at(t, TILE)
            up = dot_nn(buf[at, :], up_v[:, cols])
            d_act = dot_nt(g_v[at, :], down_v[cols, :])
            half = 0.5 * (1.0 + lax.erf(up * ROOT_HALF))
            act_v[at, cols] = (up * half).astype(BF16)
            slope = half + up * jnp.exp(-0.5 * up * up) * INV_ROOT_TAU
            dup_v[at, cols] = (d_act * slope).astype(BF16)

        @pl.loop(0, model // TILE)
        def _(t):
            cols = block_at(t, TILE)
            part[at, cols] = dot_nt(dup_v[at, :], up_v[cols, :]).astype(BF16)

    def compute_down(j):
        at = block_at(j, rows)

        @pl.loop(0, model // TILE)
        def _(t):
            cols = block_at(t, TILE)
            mlp_v[at, cols] = dot_nn(act_v[at, :], down_v[:, cols]).astype(BF16)

        for copy in stores(j):
            copy.start()

    compute(p)
    compute_down(p)

    @pl.loop(1, n)
    def _(s):
        for c in range(PARTS):
            gather.step(s, c)

        @pl.when(p - s >= 0)
        def _():
            compute(p - s)

            @pl.when(p == n - 1)
            def _():
                for c in range(PARTS):
                    scatter.send_left(p - s, c)

            compute_down(p - s)

        @pl.when(p + s < n)
        def _():
            compute(p + s)

            @pl.when(p == 0)
            def _():
                for c in range(PARTS):
                    scatter.send_right(p + s, c)

            compute_down(p + s)

    @pl.loop(1, 2 * n - 2)
    def _(s):
        for c in range(PARTS):

            @pl.when(p > 0)
            def _():
                scatter.send_right(s - p, c)

            @pl.when(p < n - 1)
            def _():
                scatter.send_left(2 * (n - 1) - p - s, c)

    scatter.finish(out_v)
    store_out = pltpu.make_async_copy(out_v, dh_ref, load_sem.at[0])
    store_out.start()
    scatter.end()
    gather.end()

    @pl.loop(0, n)
    def _(j):
        for copy in stores(j):
            copy.wait()

    store_out.wait()


def feed(normed, cot_all, w_up, w_down, n):
    rows, model = normed.shape
    hidden = w_up.shape[1]
    group = n * rows
    full = pltpu.VMEM((group, model), BF16)
    wide = pltpu.VMEM((group, hidden), BF16)
    return remote_call(
        functools.partial(feed_kernel, n, rows),
        "feed",
        3,
        (
            jax.ShapeDtypeStruct((group, model), BF16),
            jax.ShapeDtypeStruct((group, hidden), BF16),
            jax.ShapeDtypeStruct((group, hidden), BF16),
            jax.ShapeDtypeStruct((group, model), BF16),
            jax.ShapeDtypeStruct((rows, model), F32),
        ),
        [
            full,
            pltpu.VMEM(w_up.shape, BF16),
            pltpu.VMEM(w_down.shape, BF16),
            full,
            wide,
            wide,
            full, full, full, full,
            pltpu.VMEM((rows, model), F32),
        ]
        + [line_sems(n)] * 7
        + [pltpu.SemaphoreType.DMA((4,)), pltpu.SemaphoreType.DMA((4, n))],
        140,
        normed,
        cot_all,
        w_up,
        w_down,
    )


def unbranch_kernel(
    n, rows, d_ref, w_ref, mlp_ref, all_ref, da_ref, out_ref,
    buf, w_v, a_v, part, from_left, from_right, out_v,
    gr_sem, gl_sem, grecv_sem, sr_sem, sl_sem, lrecv_sem, rrecv_sem, load_sem, store_sem,
):
    line = Line(n, rows)
    p = line.p
    width, model = w_v.shape
    loads = (
        pltpu.make_async_copy(d_ref, line.shard(buf, p), load_sem.at[0]),
        pltpu.make_async_copy(mlp_ref, part, load_sem.at[1]),
        pltpu.make_async_copy(w_ref, w_v, load_sem.at[2]),
    )
    for copy in loads:
        copy.start()
    line_enter(p, n)
    for copy in loads:
        copy.wait()
    gather = Gather(line, buf, gr_sem, gl_sem, grecv_sem)
    scatter = Scatter(line, part, from_left, from_right, sr_sem, sl_sem, lrecv_sem, rrecv_sem)
    gather.begin()

    def compute(j):
        at = block_at(j, rows)

        @pl.loop(0, width // TILE)
        def _(t):
            cols = block_at(t, TILE)
            a_v[at, cols] = dot_nt(buf[at, :], w_v[cols, :]).astype(BF16)

    @pl.loop(0, n)
    def _(s):
        for c in range(PARTS):

            @pl.when(s > 0)
            def _():
                gather.step(s, c)

            scatter.send_right(n - 1 - s, c)
            scatter.send_left(s, c)

        @pl.when(p - s >= 0)
        def _():
            compute(p - s)

        @pl.when((p + s < n) & (s > 0))
        def _():
            compute(p + s)

    scatter.finish(out_v)
    stores = (
        pltpu.make_async_copy(out_v, out_ref, store_sem.at[0]),
        pltpu.make_async_copy(buf, all_ref, store_sem.at[1]),
        pltpu.make_async_copy(a_v, da_ref, store_sem.at[2]),
    )
    for copy in stores:
        copy.start()
    scatter.end()
    gather.end()
    for copy in stores:
        copy.wait()


def unbranch(d_branch, w_out, mlp_part, n):
    rows, model = d_branch.shape
    group = n * rows
    width = w_out.shape[0]
    full = pltpu.VMEM((group, model), BF16)
    return remote_call(
        functools.partial(unbranch_kernel, n, rows),
        "unbranch",
        4,
        (
            jax.ShapeDtypeStruct((group, model), BF16),
            jax.ShapeDtypeStruct((group, width), BF16),
            jax.ShapeDtypeStruct((rows, model), F32),
        ),
        [
            full,
            pltpu.VMEM(w_out.shape, BF16),
            pltpu.VMEM((group, width), BF16),
            full, full, full,
            pltpu.VMEM((rows, model), F32),
        ]
        + [line_sems(n)] * 7
        + [pltpu.SemaphoreType.DMA((3,)), pltpu.SemaphoreType.DMA((3,))],
        100,
        d_branch,
        w_out,
        mlp_part,
    )


def unproject_kernel(
    n, rows, d_ref, w_ref, out_ref,
    d_v, w_v, part, from_left, from_right, out_v,
    sr_sem, sl_sem, lrecv_sem, rrecv_sem, load_sem,
):
    line = Line(n, rows)
    p = line.p
    model = w_v.shape[1]
    loads = (
        pltpu.make_async_copy(d_ref, d_v, load_sem.at[0]),
        pltpu.make_async_copy(w_ref, w_v, load_sem.at[1]),
    )
    for copy in loads:
        copy.start()
    line_enter(p, n)
    for copy in loads:
        copy.wait()
    scatter = Scatter(line, part, from_left, from_right, sr_sem, sl_sem, lrecv_sem, rrecv_sem)

    def compute(j):
        at = block_at(j, rows)

        @pl.loop(0, model // TILE)
        def _(t):
            cols = block_at(t, TILE)
            total = dot_nt(d_v[0, at, :], w_v[0, cols, :])
            total += dot_nt(d_v[1, at, :], w_v[1, cols, :])
            total += dot_nt(d_v[2, at, :], w_v[2, cols, :])
            part[at, cols] = total.astype(BF16)

    @pl.loop(0, n)
    def _(s):
        right, left = n - 1 - s, s

        @pl.when(right > p)
        def _():
            compute(right)

        @pl.when(left < p)
        def _():
            compute(left)

        for c in range(PARTS):
            scatter.send_right(right, c)
            scatter.send_left(left, c)

    compute(p)
    scatter.finish(out_v)
    store = pltpu.make_async_copy(out_v, out_ref, load_sem.at[0])
    store.start()
    scatter.end()
    store.wait()


def unproject(d_qkv, weights, rows, n):
    model = weights.shape[1]
    group = n * rows
    full = pltpu.VMEM((group, model), BF16)
    return remote_call(
        functools.partial(unproject_kernel, n, rows),
        "unproject",
        5,
        jax.ShapeDtypeStruct((rows, model), F32),
        [
            pltpu.VMEM(d_qkv.shape, BF16),
            pltpu.VMEM(weights.shape, BF16),
            full, full, full,
            pltpu.VMEM((rows, model), F32),
        ]
        + [line_sems(n)] * 4
        + [pltpu.SemaphoreType.DMA((2,))],
        80,
        d_qkv,
        weights,
    )


def fill_bias(bias, slope, length):
    row = lax.broadcasted_iota(jnp.int32, bias.shape, 0)
    bias[...] = jnp.where(row < length, slope * row.astype(F32), MASKED)


def causal_tile():
    shape = (TILE, TILE)
    return lax.broadcasted_iota(jnp.int32, shape, 0) <= lax.broadcasted_iota(jnp.int32, shape, 1)


def attend_kernel(len_ref, slope_ref, q_ref, k_ref, v_ref, out_ref, lse_ref, bias, vt_v):
    pair = pl.program_id(0)
    slots = q_ref.shape[0]
    lane = lax.broadcasted_iota(jnp.int32, (TILE, LANES), 1)
    causal = causal_tile()
    vt_v[...] = v_ref[...].T
    for h in range(2):
        mine = (lane >= HEAD_DIM) if h else (lane < HEAD_DIM)
        fill_bias(bias, slope_ref[pair * 2 + h], len_ref[0])
        for b in range(slots // TILE):
            at = slice(b * TILE, (b + 1) * TILE)
            end = (b + 1) * TILE
            query = jnp.where(mine, q_ref[at, :] * 0.125, 0).astype(BF16)
            last = dot_nt(k_ref[at, :], query) + bias[at, :]
            last = jnp.where(causal, last, MASKED)
            top = jnp.max(last, axis=0, keepdims=True)
            if b > 0:
                first = dot_nt(k_ref[: b * TILE, :], query) + bias[: b * TILE, :]
                top = jnp.maximum(top, jnp.max(first, axis=0, keepdims=True))
            probs = jnp.exp(last - top)
            total = jnp.sum(probs, axis=0, keepdims=True)
            mixed = dot_nn(vt_v[:, at], probs.astype(BF16))
            if b > 0:
                probs = jnp.exp(first - top)
                total += jnp.sum(probs, axis=0, keepdims=True)
                mixed += dot_nn(vt_v[:, : b * TILE], probs.astype(BF16))
            value = (mixed / total).T.astype(BF16)
            if h:
                out_ref[at, :] = jnp.where(mine, value, out_ref[at, :])
            else:
                out_ref[at, :] = value
            lse_ref[0, h : h + 1, at] = top + jnp.log(total)


def attend(qkv, slopes, lengths):
    _, slots, width = qkv.shape
    pairs = width // LANES

    def spec(i):
        return pl.BlockSpec((pl.Squeezed(), slots, LANES), lambda g, *_: (i, 0, g))

    return pl.pallas_call(
        attend_kernel,
        name="attend",
        out_shape=(
            jax.ShapeDtypeStruct((slots, width), BF16),
            jax.ShapeDtypeStruct((pairs, 2, slots), F32),
        ),
        grid_spec=pltpu.PrefetchScalarGridSpec(
            num_scalar_prefetch=2,
            grid=(pairs,),
            in_specs=[spec(0), spec(1), spec(2)],
            out_specs=(
                pl.BlockSpec((slots, LANES), lambda g, *_: (0, g)),
                pl.BlockSpec((1, 2, slots), lambda g, *_: (g, 0, 0)),
            ),
            scratch_shapes=[pltpu.VMEM((slots, TILE), F32), pltpu.VMEM((LANES, slots), BF16)],
        ),
        cost_estimate=pl.CostEstimate(flops=int(2e10), bytes_accessed=1 << 22, transcendentals=0),
        compiler_params=pltpu.CompilerParams(vmem_limit_bytes=VMEM_BYTES),
    )(lengths, slopes, qkv, qkv, qkv)


def unattend_kernel(
    len_ref, slope_ref, q_ref, k_ref, v_ref, do_ref, lse_ref, out_ref, bias, kt_v, dk_v, dv_v
):
    pair = pl.program_id(0)
    slots = q_ref.shape[0]
    lane = lax.broadcasted_iota(jnp.int32, (TILE, LANES), 1)
    causal = causal_tile()
    kt_v[...] = k_ref[...].T
    dk_v[...] = jnp.zeros_like(dk_v)
    dv_v[...] = jnp.zeros_like(dv_v)
    for h in range(2):
        mine = (lane >= HEAD_DIM) if h else (lane < HEAD_DIM)
        fill_bias(bias, slope_ref[pair * 2 + h], len_ref[0])
        for b in range(slots // TILE):
            at = slice(b * TILE, (b + 1) * TILE)
            query = jnp.where(mine, q_ref[at, :] * 0.125, 0).astype(BF16)
            grad = jnp.where(mine, do_ref[at, :], 0).astype(BF16)
            lse = lse_ref[0, h : h + 1, at]
            spans = [at] + ([slice(0, b * TILE)] if b else [])
            kept = []
            weighted = jnp.zeros((1, TILE), F32)
            for i, span in enumerate(spans):
                scores = dot_nt(k_ref[span, :], query) + bias[span, :]
                if i == 0:
                    scores = jnp.where(causal, scores, MASKED)
                probs = jnp.exp(scores - lse)
                d_probs = dot_nt(v_ref[span, :], grad)
                weighted += jnp.sum(probs * d_probs, axis=0, keepdims=True)
                kept.append((probs, d_probs))
                dv_v[span, :] += dot_nn(probs.astype(BF16), grad)
            d_query = jnp.zeros((LANES, TILE), F32)
            for span, (probs, d_probs) in zip(spans, kept):
                d_scores = (probs * (d_probs - weighted)).astype(BF16)
                dk_v[span, :] += dot_nn(d_scores, query)
                d_query += dot_nn(kt_v[:, span], d_scores)
            value = (d_query * 0.125).T.astype(BF16)
            if h:
                out_ref[0, at, :] = jnp.where(mine, value, out_ref[0, at, :])
            else:
                out_ref[0, at, :] = value
    out_ref[1, :, :] = dk_v[...].astype(BF16)
    out_ref[2, :, :] = dv_v[...].astype(BF16)


def unattend(qkv, d_attn, lse, slopes, lengths):
    _, slots, width = qkv.shape
    pairs = width // LANES

    def spec(i):
        return pl.BlockSpec((pl.Squeezed(), slots, LANES), lambda g, *_: (i, 0, g))

    return pl.pallas_call(
        unattend_kernel,
        name="unattend",
        out_shape=jax.ShapeDtypeStruct(qkv.shape, BF16),
        grid_spec=pltpu.PrefetchScalarGridSpec(
            num_scalar_prefetch=2,
            grid=(pairs,),
            in_specs=[
                spec(0),
                spec(1),
                spec(2),
                pl.BlockSpec((slots, LANES), lambda g, *_: (0, g)),
                pl.BlockSpec((1, 2, slots), lambda g, *_: (g, 0, 0)),
            ],
            out_specs=pl.BlockSpec((3, slots, LANES), lambda g, *_: (0, 0, g)),
            scratch_shapes=[
                pltpu.VMEM((slots, TILE), F32),
                pltpu.VMEM((LANES, slots), BF16),
                pltpu.VMEM((slots, LANES), F32),
                pltpu.VMEM((slots, LANES), F32),
            ],
        ),
        cost_estimate=pl.CostEstimate(flops=int(3e10), bytes_accessed=1 << 22, transcendentals=0),
        compiler_params=pltpu.CompilerParams(vmem_limit_bytes=VMEM_BYTES),
    )(lengths, slopes, qkv, qkv, qkv, d_attn, lse)


def norm_sum_kernel(nd, nt, x_ref, out_ref, from_t, total, from_d, t_send, t_recv, d_send, d_recv):
    d, t = lax.axis_index("dp"), lax.axis_index("tensor")
    barrier = pltpu.get_barrier_semaphore()
    for i in range(1, nt):
        peer = lax.rem(t + i, nt)
        pl.semaphore_signal(barrier, inc=1, device_id={"tensor": peer}, device_id_type=MESH)
    for i in range(1, nd):
        peer = lax.rem(d + i, nd)
        pl.semaphore_signal(barrier, inc=1, device_id={"dp": peer}, device_id_type=MESH)
    pl.semaphore_wait(barrier, nt + nd - 2)
    first = []
    for i in range(1, nt):
        peer = lax.rem(t + i, nt)
        first.append(
            pltpu.make_async_remote_copy(
                src_ref=x_ref.at[peer],
                dst_ref=from_t.at[i - 1],
                send_sem=t_send.at[i - 1],
                recv_sem=t_recv.at[i - 1],
                device_id={"tensor": peer},
                device_id_type=MESH,
            )
        )
    for copy in first:
        copy.start()
    total[...] = x_ref[t]
    for i, copy in enumerate(first):
        copy.wait_recv()
        total[...] += from_t[i]
    second = []
    for i in range(1, nd):
        peer = lax.rem(d + i, nd)
        second.append(
            pltpu.make_async_remote_copy(
                src_ref=total.at[peer],
                dst_ref=from_d.at[i - 1],
                send_sem=d_send.at[i - 1],
                recv_sem=d_recv.at[i - 1],
                device_id={"dp": peer},
                device_id_type=MESH,
            )
        )
    for copy in second:
        copy.start()
    out_ref[...] = total[d]
    for i, copy in enumerate(second):
        copy.wait_recv()
        out_ref[...] += from_d[i]
    for copy in first + second:
        copy.wait_send()


def norm_sum(local, nd, nt):
    lanes = local.shape[1] // (nd * nt)
    x = local.reshape(4, nd, nt, lanes).transpose(2, 1, 0, 3)
    x = jnp.pad(x, ((0, 0), (0, 0), (0, 4), (0, LANES - lanes)))
    vmem = pl.BlockSpec(memory_space=pltpu.VMEM)
    out = pl.pallas_call(
        functools.partial(norm_sum_kernel, nd, nt),
        name="norm_sum",
        out_shape=jax.ShapeDtypeStruct((8, LANES), F32),
        in_specs=[vmem],
        out_specs=vmem,
        scratch_shapes=[
            pltpu.VMEM((nt - 1, nd, 8, LANES), F32),
            pltpu.VMEM((nd, 8, LANES), F32),
            pltpu.VMEM((nd - 1, 8, LANES), F32),
            pltpu.SemaphoreType.DMA((nt - 1,)),
            pltpu.SemaphoreType.DMA((nt - 1,)),
            pltpu.SemaphoreType.DMA((nd - 1,)),
            pltpu.SemaphoreType.DMA((nd - 1,)),
        ],
        compiler_params=pltpu.CompilerParams(collective_id=6, has_side_effects=True),
    )(x)
    return out[:4, :lanes]


def per_device(tokens, w_qkv, w_out, w_up, w_down, norm_gains, norm_biases, lengths, cotangent):
    rows = tokens.shape[0]
    n, nd = lax.axis_size("tensor"), lax.axis_size("dp")
    norms = lax.all_gather(
        jnp.concatenate([norm_gains, norm_biases]).astype(BF16), "dp", axis=1, tiled=True
    ).astype(F32)
    gains, shifts = norms[:2], norms[2:]
    qkv_all = lax.all_gather(w_qkv.astype(BF16), "dp", axis=1, tiled=True)
    out_all = lax.all_gather(w_out.astype(BF16), "dp", axis=1, tiled=True)
    up_all = lax.all_gather(w_up.astype(BF16), "dp", axis=0, tiled=True)
    down_all = lax.all_gather(w_down.astype(BF16), "dp", axis=1, tiled=True)
    t = lax.axis_index("tensor")
    heads_local = qkv_all.shape[2] // HEAD_DIM
    head_ids = (t * heads_local + jnp.arange(heads_local, dtype=jnp.int32)).astype(F32)
    slopes = jnp.exp2(-8.0 * (head_ids + 1.0) / (heads_local * n))
    live_rows = (t * rows + jnp.arange(rows, dtype=jnp.int32) < lengths[0])[:, None]
    inputs = tokens.astype(F32)
    hat_one, inv_one = normalize(inputs)
    normed_one = (hat_one * gains[0] + shifts[0]).astype(BF16)
    qkv, normed_one_all = project(normed_one, qkv_all, n)
    attn, lse = attend(qkv, slopes, lengths)
    masked_cot = jnp.where(live_rows, cotangent, jnp.zeros_like(cotangent))
    attn_branch, masked_cot_all = branch(attn, out_all, masked_cot, n)
    after_attn = inputs + attn_branch
    hat_two, inv_two = normalize(after_attn)
    normed_two = (hat_two * gains[1] + shifts[1]).astype(BF16)
    normed_two_all, activated, d_up, mlp_part, d_norm_two = feed(
        normed_two, masked_cot_all, up_all, down_all, n
    )
    gain_two = jnp.sum(d_norm_two * hat_two, axis=0)
    shift_two = jnp.sum(d_norm_two, axis=0)
    d_after = masked_cot.astype(F32) + norm_back(d_norm_two, hat_two, inv_two, gains[1])
    d_branch = d_after.astype(BF16)
    grad_down = dot_tn(activated, masked_cot_all).astype(BF16)
    down_shard = lax.psum_scatter(grad_down, "dp", scatter_dimension=1, tiled=True).astype(F32)
    grad_up = dot_tn(normed_two_all, d_up).astype(BF16)
    up_shard = lax.psum_scatter(grad_up, "dp", scatter_dimension=0, tiled=True).astype(F32)
    d_branch_all, d_attn, mlp_branch = unbranch(d_branch, out_all, mlp_part, n)
    output = jnp.where(live_rows, after_attn + mlp_branch, 0.0).astype(BF16)
    grad_out = dot_tn(attn, d_branch_all).astype(BF16)
    out_shard = lax.psum_scatter(grad_out, "dp", scatter_dimension=1, tiled=True).astype(F32)
    d_qkv = unattend(qkv, d_attn, lse, slopes, lengths)
    grad_qkv = jnp.stack([dot_tn(normed_one_all, d_qkv[i]) for i in range(3)]).astype(BF16)
    qkv_shard = lax.psum_scatter(grad_qkv, "dp", scatter_dimension=1, tiled=True).astype(F32)
    d_norm_one = unproject(d_qkv, qkv_all, rows, n)
    gain_one = jnp.sum(d_norm_one * hat_one, axis=0)
    shift_one = jnp.sum(d_norm_one, axis=0)
    input_grad = (d_after + norm_back(d_norm_one, hat_one, inv_one, gains[0])).astype(BF16)
    sums = norm_sum(jnp.stack([gain_one, gain_two, shift_one, shift_two]), nd, n)
    return (output, input_grad, qkv_shard, out_shard, up_shard, down_shard, sums[:2], sums[2:])


def solution(mesh):
    placed = (
        P(("dp", "tensor"), None),
        P(None, "dp", "tensor"),
        P("tensor", "dp"),
        P("dp", "tensor"),
        P("tensor", "dp"),
        P(None, "dp"),
        P(None, "dp"),
        P("dp"),
        P(("dp", "tensor"), None),
    )
    return jax.shard_map(
        per_device,
        mesh=mesh,
        in_specs=placed,
        out_specs=(
            P(("dp", "tensor"), None),
            P(("dp", "tensor"), None),
            P(None, "dp", "tensor"),
            P("tensor", "dp"),
            P("dp", "tensor"),
            P("tensor", "dp"),
            P(None, ("dp", "tensor")),
            P(None, ("dp", "tensor")),
        ),
        check_vma=False,
    )
```

time: 1540 us -> 798 us (0.52)
  waiting for transfers between devices: 1190 us -> 109 us
  Pallas kernels: 0 us -> 563 us
  matrix products: 233 us -> 44.8 us
  other arithmetic: 60.9 us -> 40.9 us
    pallas_call x0 -> x8, Pallas kernels: none -> 563 us  [the longest x5 501 us: remote_call(): pl.pallas_call(body, name=name, out_shape=outs, in_specs=[ANY] * len(args...]
    all_gather x8 -> x4, waiting for transfers between devices: 440 us -> 28.1 us  [the longest x1 28.1 us: per_device(): qkv_all = lax.all_gather(w_qkv.astype(BF16), 'dp', axis=1, tiled=True)]
    reduce_scatter x8 -> x4, waiting for transfers between devices: 478 us -> 80.4 us  [the longest x1 72.3 us: per_device(): lax.psum_scatter(grad_up, 'dp', scatter_dimension=0, tiled=True).astype(F32)]
    unnamed x20 -> x8, waiting for transfers between devices: 270 us -> 0.13 us
    dot_general x28 -> x6, matrix products: 213 us -> 44.8 us  [dot_tn(): lax.dot_general(left, right, (((0,), (0,)), ((), ())), preferred_element_...]
    sub x2 -> x0, matrix products: 20.3 us -> none  [attention_forward(): weights = jnp.exp(scores - row_top)]
    convert_element_type x18 -> x13, other arithmetic: 40.5 us -> 27 us  [the longest x1 2.94 us: per_device(): output = jnp.where(live_rows, after_attn + mlp_branch, 0.0).astype(BF16)]
  transfers between devices with their start and end apart: 18 -> 8, of which waited for: 17 -> 3; matrix products, arithmetic and copies ran while one was open for 12% -> 9% of each run, Pallas kernels for 0% -> 42%
where the time goes in v1:
time: 798 us; the launch traced here: 790 us
  Pallas kernels  563 us (71%)
  waiting for transfers between devices  109 us (14%)
  matrix products  44.8 us (6%)
  other arithmetic  40.9 us (5%)
  between operations  15.8 us (2%)
  blocking collectives  10.6 us (1%)
    pallas_call x5, Pallas kernels, remote_call(): pl.pallas_call(body, name=name, out_shape=outs, in_specs=[ANY] * len(args...  501 us
    reduce_scatter x1, waiting for transfers between devices, per_device(): lax.psum_scatter(grad_up, 'dp', scatter_dimension=0, tiled=True).astype(F32)  72.3 us
    dot_general x6, matrix products, dot_tn(): lax.dot_general(left, right, (((0,), (0,)), ((), ())), preferred_element_...  44.8 us
    all_gather x1, waiting for transfers between devices, per_device(): qkv_all = lax.all_gather(w_qkv.astype(BF16), 'dp', axis=1, tiled=True)  28.1 us
    pallas_call x1, Pallas kernels, norm_sum(): pl.pallas_call(functools.partial(norm_sum_kernel, nd, nt), name='norm_sum...  23.3 us
    pallas_call x1, Pallas kernels, unattend(): pl.pallas_call(unattend_kernel, name='unattend', out_shape=jax.ShapeDtype...  23.1 us
  transfers between devices with their start and end apart: 8, of which 3 were waited for; matrix products, arithmetic and copies ran while one was open for 9% of the time, Pallas kernels for 42%

profile of v1, /device:TPU:0, one launch (start us, length us, event | category | flops | bytes accessed | tf_op | source)
XLA Modules:
  0.0 789.8 jit_solution(3447414059980566292)
XLA Ops:
  7.2 2.5 convert_element_type.68
  11.9 2.7 convert_element_type.73
  16.8 10.6 %all_gather.15 = bf16[4,2048]{1,0:T(4,128)(2,1)S(1)} all-gather(bf16[4,256]{1,0:T(4,128)(2,1)S(1)} %pad_maximum_fusion.1), channel_id=1, replica_groups=mesh['dp'=8,'tensor'=4] {'dp'}, dimensions={1}, use_global_device_ids=true | all-gather | bytes 18432 | tf_op jit(solution)/shard_map/all_gather | solution.py:992
  29.1 1.4 fusion.10.h_ref
  30.6 28.1 %all-gather.5.cloned.1.call-done.w_ref = bf16[3,2048,512]{2,1,0:T(8,128)(2,1)} async-done(((bf16[3,256,512]{2,1,0:T(8,128)(2,1)}), bf16[3,2048,512]{2,1,0:T(8,128)(2,1)}) %all-gather.5.cloned.1.call-update) | async-done | bytes 6291472 | tf_op jit(solution)/shard_map/all_gather | solution.py:996
  58.7 75.3 %project.1 = (bf16[3,1024,512]{2,1,0:T(8,128)(2,1)}, bf16[1024,2048]{1,0:T(8,128)(2,1)}) custom-call(bf16[256,2048]{1,0:T(8,128)(2,1)} %fusion.10.h_ref, bf16[3,2048,512]{2,1,0:T(8,128)(2,1)} %all-gather.5.cloned.1.call-done.w_ref), custom_call_target="tpu_custom_call" | custom-call | flops 89699999744 | bytes 1048576 | tf_op jit(solution)/shard_map/project/pallas_call | solution.py:247
  134.0 15.7 %attend.1 = (bf16[1024,512]{1,0:T(8,128)(2,1)}, f32[4,2,1024]{2,1,0:T(2,128)}) custom-call(s32[1]{0:T(128)} %copy.21.len_ref, f32[8]{0:T(128)} %multiply_exponential_fusion.slope_ref, bf16[3,1024,512]{2,1,0:T(8,128)(2,1)} %get-tuple-element.22.q_ref.k_ref.v_ref, bf16[3,1024,512]{2,1,0:T(8,128)(2,1)} %get-tuple-element.22.q_ref.k_ref.v_ref, ...), custom_call_target="tpu_custom_call" | custom-call | flops 20000000000 | bytes 4194304 | tf_op jit(solution)/shard_map/attend/pallas_call | solution.py:812
  149.8 122.5 %branch.1 = (f32[256,2048]{1,0:T(8,128)}, bf16[1024,2048]{1,0:T(8,128)(2,1)}) custom-call(bf16[1024,512]{1,0:T(8,128)(2,1)} %get-tuple-element.23.attn_ref, bf16[512,2048]{1,0:T(8,128)(2,1)} %all-gather.7.cloned.1.call-done.w_ref, bf16[256,2048]{1,0:T(8,128)(2,1)} %broadcast_select_fusion.g_ref), custom_call_target="tpu_custom_call" | custom-call | flops 115000000512 | bytes 1048576 | tf_op jit(solution)/shard_map/branch/pallas_call | solution.py:247
  272.2 1.9 fusion.19
  276.9 115.9 %feed.1 = (bf16[1024,2048]{1,0:T(8,128)(2,1)}, bf16[1024,2048]{1,0:T(8,128)(2,1)}, bf16[1024,2048]{1,0:T(8,128)(2,1)}, bf16[1024,2048]{1,0:T(8,128)(2,1)}, f32[256,2048]{1,0:T(8,128)}) custom-call(bf16[256,2048]{1,0:T(8,128)(2,1)} %add_convert_fusion.h_ref, bf16[1024,2048]{1,0:T(8,128)(2,1)} %get-tuple-element.25.g_ref, ...), custom_call_target="tpu_custom_call" | custom-call | flops 160999997440 | bytes 1048576 | tf_op jit(solution)/shard_map/feed/pallas_call | solution.py:247
  392.9 3.2 multiply_reduce_fusion
  396.2 2.5 fusion.18
  398.7 119.5 %unbranch.1 = (bf16[1024,2048]{1,0:T(8,128)(2,1)}, bf16[1024,512]{1,0:T(8,128)(2,1)}, f32[256,2048]{1,0:T(8,128)}) custom-call(bf16[256,2048]{1,0:T(8,128)(2,1)} %get-tuple-element.44.d_ref, bf16[512,2048]{1,0:T(8,128)(2,1)} %all-gather.7.cloned.1.call-done.w_ref, bf16[1024,2048]{1,0:T(8,128)(2,1)} %get-tuple-element.27.mlp_ref), custom_call_target="tpu_custom_call" | custom-call | flops 115000000512 | bytes 1048576 | tf_op jit(solution)/shard_map/unbranch/pallas_call | solution.py:247
  518.3 5.9 convolution_convert_fusion.2
  524.4 23.1 %unattend.1.d_ref = bf16[3,1024,512]{2,1,0:T(8,128)(2,1)} custom-call(s32[1]{0:T(128)} %copy.21.len_ref, f32[8]{0:T(128)} %multiply_exponential_fusion.slope_ref, bf16[3,1024,512]{2,1,0:T(8,128)(2,1)} %get-tuple-element.22.q_ref.k_ref.v_ref, bf16[3,1024,512]{2,1,0:T(8,128)(2,1)} %get-tuple-element.22.q_ref.k_ref.v_ref, ...), custom_call_target="tpu_custom_call" | custom-call | flops 30000001024 | bytes 4194304 | tf_op jit(solution)/shard_map/unattend/pallas_call | solution.py:885
  547.5 5.1 fusion.2
  552.6 2.4 fusion.1
  555.0 2.4 fusion
  557.5 3.2 pad_maximum_fusion
  561.0 14.1 %convolution_convert_fusion = bf16[2048,2048]{1,0:T(8,128)(2,1)} fusion(bf16[1024,2048]{1,0:T(8,128)(2,1)} %get-tuple-element.35, bf16[1024,2048]{1,0:T(8,128)(2,1)} %get-tuple-element.25.g_ref), kind=kOutput, calls=%fused_computation | convolution fusion | flops 8594128896 | bytes 16777216 | tf_op jit(solution)/shard_map/dot_general | solution.py:36
  575.2 14.9 %convolution_convert_fusion.1 = bf16[2048,2048]{1,0:T(8,128)(2,1)} fusion(bf16[1024,2048]{1,0:T(8,128)(2,1)} %get-tuple-element.33, bf16[1024,2048]{1,0:T(8,128)(2,1)} %get-tuple-element.34), kind=kOutput, calls=%fused_computation.1 | convolution fusion | flops 8594128896 | bytes 16777216 | tf_op jit(solution)/shard_map/dot_general | solution.py:36
  591.0 67.9 %unproject.1 = f32[256,2048]{1,0:T(8,128)} custom-call(bf16[3,1024,512]{2,1,0:T(8,128)(2,1)} %unattend.1.d_ref, bf16[3,2048,512]{2,1,0:T(8,128)(2,1)} %all-gather.5.cloned.1.call-done.w_ref), custom_call_target="tpu_custom_call" | custom-call | flops 92000002048 | bytes 1048576 | tf_op jit(solution)/shard_map/unproject/pallas_call | solution.py:247
  659.0 2.7 fusion.16
  662.7 23.3 %norm_sum.1 = f32[8,128]{1,0:T(8,128)} custom-call(f32[4,8,8,128]{3,2,1,0:T(8,128)} %pad.4.x_ref), custom_call_target="tpu_custom_call" | custom-call | tf_op jit(solution)/shard_map/norm_sum/pallas_call | solution.py:969
  687.4 2.9 select_convert_fusion
  690.5 1.8 fusion.15
  692.4 1.8 convert_element_type.79
  694.1 2.5 convert_element_type.77
  696.6 8.1 %reduce-scatter.11.cloned.1.call-done = bf16[2048,256]{1,0:T(8,128)(2,1)} async-done(((bf16[2048,2048]{1,0:T(8,128)(2,1)}), bf16[2048,256]{1,0:T(8,128)(2,1)}) %reduce-scatter.11.cloned.1.call-update) | async-done | bytes 1048592 | tf_op jit(solution)/shard_map/reduce_scatter | solution.py:1023
  704.7 2.7 convert_element_type.83
  707.4 72.3 %reduce-scatter.9.cloned.1.call-done = bf16[256,2048]{1,0:T(8,128)(2,1)} async-done(((bf16[2048,2048]{1,0:T(8,128)(2,1)}), bf16[256,2048]{1,0:T(8,128)(2,1)}) %reduce-scatter.9.cloned.1.call-update) | async-done | bytes 1048592 | tf_op jit(solution)/shard_map/reduce_scatter | solution.py:1025
  779.7 2.8 convert_element_type.81
  (124 shorter events, 12.0 us)
Async XLA Ops:
  7.2 3.5 copy-start.11
  7.2 51.5 %all-gather.5.cloned.1.call-start = ((), (), s32[]{:S(2)}) async-start(), calls=%async_computation.4 | async-start | bytes 7077888 | tf_op jit(solution)/shard_map/all_gather | solution.py:996
  9.8 140.0 %all-gather.7.cloned.1.call-start = ((), (), s32[]{:S(2)}) async-start(), calls=%async_computation.5 | async-start | bytes 2359296 | tf_op jit(solution)/shard_map/all_gather | solution.py:997
  10.6 266.3 %all-gather.9.cloned.1.call-start = ((), (), s32[]{:S(2)}) async-start(), calls=%async_computation.6 | async-start | bytes 9437184 | tf_op jit(solution)/shard_map/all_gather | solution.py:998
  11.8 4.2 copy-start.31
  11.8 4.2 copy-start.32
  11.8 4.2 copy-start.3
  11.8 265.1 %all-gather.11.cloned.1.call-start = ((), (), s32[]{:S(2)}) async-start(), calls=%async_computation.7 | async-start | bytes 9437184 | tf_op jit(solution)/shard_map/all_gather | solution.py:999
  14.6 13.3 %copy-start.9 = (bf16[256,2048]{1,0:T(8,128)(2,1)S(1)}, bf16[256,2048]{1,0:T(8,128)(2,1)}, u32[]{:S(2)}) copy-start(bf16[256,2048]{1,0:T(8,128)(2,1)} %param.17) | copy-start | bytes 3145732
  14.7 677.7 %reduce-scatter.7.cloned.1.call-start = ((), (), s32[]{:S(2)}) async-start(), calls=%async_computation.9 | async-start | bytes 2359296 | tf_op jit(solution)/shard_map/reduce_scatter | solution.py:1029
  16.3 12.8 %copy-start.22 = (f32[256]{0:T(256)}, f32[256]{0:T(256)S(1)}, u32[]{:S(2)}) copy-start(f32[256]{0:T(256)S(1)} %broadcast_multiply_fusion.5) | copy-start | bytes 3076
  16.8 12.4 %copy-start.26 = (f32[256]{0:T(256)}, f32[256]{0:T(256)S(1)}, u32[]{:S(2)}) copy-start(f32[256]{0:T(256)S(1)} %add_rsqrt_fusion.1) | copy-start | bytes 3076
  149.7 122.5 %copy-start.4 = (bf16[256,2048]{1,0:T(8,128)(2,1)S(1)}, bf16[256,2048]{1,0:T(8,128)(2,1)}, u32[]{:S(2)}) copy-start(bf16[256,2048]{1,0:T(8,128)(2,1)} %param.9) | copy-start | bytes 3145732
  276.9 116.0 %copy-start.1 = (f32[256,2048]{1,0:T(8,128)S(1)}, f32[256,2048]{1,0:T(8,128)}, u32[]{:S(2)}) copy-start(f32[256,2048]{1,0:T(8,128)} %copy-done) | copy-start | bytes 6291460
  276.9 116.0 %copy-start.16 = (f32[1,2048]{1,0:T(1,128)S(1)}, f32[1,2048]{1,0:T(1,128)}, u32[]{:S(2)}) copy-start(f32[1,2048]{1,0:T(1,128)} %get-tuple-element.48) | copy-start | bytes 24580
  276.9 116.0 %copy-start.21 = (f32[256]{0:T(256)S(1)}, f32[256]{0:T(256)}, u32[]{:S(2)}) copy-start(f32[256]{0:T(256)} %copy-done.20) | copy-start | bytes 3076
  276.9 116.0 %copy-start.25 = (f32[256]{0:T(256)S(1)}, f32[256]{0:T(256)}, u32[]{:S(2)}) copy-start(f32[256]{0:T(256)} %copy-done.24) | copy-start | bytes 3076
  392.9 3.3 copy-start.6
  392.9 3.3 copy-start.10
  392.9 3.3 copy-start.29
  398.7 119.5 %copy-start.33 = (bf16[1024,512]{1,0:T(8,128)(2,1)S(1)}, bf16[1024,512]{1,0:T(8,128)(2,1)}, u32[]{:S(2)}) copy-start(bf16[1024,512]{1,0:T(8,128)(2,1)} %get-tuple-element.23.attn_ref) | copy-start | bytes 3145732
  524.2 170.0 %reduce-scatter.5.cloned.1.call-start = ((), (), s32[]{:S(2)}) async-start(), calls=%async_computation.8 | async-start | bytes 7077888 | tf_op jit(solution)/shard_map/reduce_scatter | solution.py:1032
  547.5 5.1 copy-start.34
  547.5 5.1 copy-start.35
  560.7 144.0 %reduce-scatter.11.cloned.1.call-start = ((), (), s32[]{:S(2)}) async-start(), calls=%async_computation.11 | async-start | bytes 9437184 | tf_op jit(solution)/shard_map/reduce_scatter | solution.py:1023
  575.1 204.6 %reduce-scatter.9.cloned.1.call-start = ((), (), s32[]{:S(2)}) async-start(), calls=%async_computation.10 | async-start | bytes 9437184 | tf_op jit(solution)/shard_map/reduce_scatter | solution.py:1025
  591.0 68.0 %copy-start.5 = (bf16[256,2048]{1,0:T(8,128)(2,1)S(1)}, bf16[256,2048]{1,0:T(8,128)(2,1)}, u32[]{:S(2)}) copy-start(bf16[256,2048]{1,0:T(8,128)(2,1)} %param.9) | copy-start | bytes 3145732
  591.0 68.0 %copy-start.14 = (f32[1,2048]{1,0:T(1,128)S(1)}, f32[1,2048]{1,0:T(1,128)}, u32[]{:S(2)}) copy-start(f32[1,2048]{1,0:T(1,128)} %copy-done.13) | copy-start | bytes 24580
  591.0 68.0 %copy-start.23 = (f32[256]{0:T(256)S(1)}, f32[256]{0:T(256)}, u32[]{:S(2)}) copy-start(f32[256]{0:T(256)} %copy-done.22) | copy-start | bytes 3076
  591.0 68.0 %copy-start.27 = (f32[256]{0:T(256)S(1)}, f32[256]{0:T(256)}, u32[]{:S(2)}) copy-start(f32[256]{0:T(256)} %copy-done.26) | copy-start | bytes 3076
  659.0 28.3 %copy-start.2 = (f32[256,2048]{1,0:T(8,128)S(1)}, f32[256,2048]{1,0:T(8,128)}, u32[]{:S(2)}) copy-start(f32[256,2048]{1,0:T(8,128)} %copy-done) | copy-start | bytes 6291460
  659.0 28.3 %copy-start.30 = (pred[256]{0:T(512)(128)(4,1)S(1)}, pred[256]{0:T(512)(128)(4,1)}, u32[]{:S(2)}) copy-start(pred[256]{0:T(512)(128)(4,1)} %copy-done.28) | copy-start | bytes 772
  (12 other events, 18.8 us)
Sparse Core Ops, SparseCore 0:
  10.5 48.1 all-gather.4
  61.1 28.0 all-gather.6
  91.7 54.2 all-gather.8
  148.3 56.0 all-gather.10
  524.3 40.3 reduce-scatter.6
  567.9 61.6 reduce-scatter.4
  633.0 71.6 reduce-scatter.10
  708.2 71.4 reduce-scatter.8

commit v2 on v1

--- a/solution.py
+++ b/solution.py
@@ -11,6 +11,7 @@
 LANES = 128
 TILE = 256
 PARTS = 4
+CHUNK = 64
 VMEM_BYTES = 60 * 1024 * 1024
 
 EPSILON = 1e-05
@@ -57,7 +58,7 @@
     return pl.ds(pl.multiple_of(index * size, size), size)
 
 
-def line_enter(p, n):
+def line_enter(p, n, more=0):
     barrier = pltpu.get_barrier_semaphore()
 
     @pl.when(p > 0)
@@ -68,7 +69,7 @@
     def _():
         pl.semaphore_signal(barrier, inc=1, device_id={"tensor": p + 1}, device_id_type=MESH)
 
-    pl.semaphore_wait(barrier, jnp.where(p > 0, 1, 0) + jnp.where(p < n - 1, 1, 0))
+    pl.semaphore_wait(barrier, jnp.where(p > 0, 1, 0) + jnp.where(p < n - 1, 1, 0) + more)
 
 
 class Line:
@@ -260,41 +261,58 @@
     )(*args)
 
 
-def project_kernel(
-    n, rows, h_ref, w_ref, qkv_ref, all_ref, buf, w_v, o_v, right_sem, left_sem, recv_sem, load_sem, q_sem, h_sem
+def gather_kernel(
+    n, nd, rows, x_ref, nrm_ref, h_ref, norms_ref,
+    buf, h_v, nrm_v, all_v, right_sem, left_sem, recv_sem, nsend_sem, nrecv_sem, load_sem, store_sem,
 ):
     line = Line(n, rows)
     p = line.p
-    width = w_v.shape[2]
-    load_w = pltpu.make_async_copy(w_ref, w_v, load_sem.at[0])
-    load_h = pltpu.make_async_copy(h_ref, line.shard(buf, p), load_sem.at[1])
-    load_h.start()
-    load_w.start()
-    line_enter(p, n)
-    load_h.wait()
+    d = lax.axis_index("dp")
+    load_x = pltpu.make_async_copy(x_ref, line.shard(buf, p), load_sem.at[0])
+    load_n = pltpu.make_async_copy(nrm_ref, nrm_v.at[d], load_sem.at[1])
+    load_x.start()
+    load_n.start()
+    barrier = pltpu.get_barrier_semaphore()
+    for i in range(1, nd):
+        peer = lax.rem(d + i, nd)
+        pl.semaphore_signal(barrier, inc=1, device_id={"dp": peer}, device_id_type=MESH)
+    line_enter(p, n, nd - 1)
+    load_x.wait()
     gather = Gather(line, buf, right_sem, left_sem, recv_sem)
     gather.begin()
-
-    def stores(j):
+    load_n.wait()
+
+    def norm_copy(i, source):
+        return pltpu.make_async_remote_copy(
+            src_ref=nrm_v.at[source],
+            dst_ref=nrm_v.at[source],
+            send_sem=nsend_sem.at[i],
+            recv_sem=nrecv_sem.at[i],
+            device_id={"dp": lax.rem(d + i, nd)},
+            device_id_type=MESH,
+        )
+
+    for i in range(1, nd):
+        norm_copy(i, d).start()
+    for i in range(1, nd):
+        norm_copy(i, lax.rem(d + nd - i, nd)).wait_recv()
+    all_v[...] = jnp.concatenate([nrm_v[i] for i in range(nd)], axis=1)
+    store_n = pltpu.make_async_copy(all_v, norms_ref, load_sem.at[0])
+    store_n.start()
+
+    def store(j):
         at = block_at(j, rows)
-        return (
-            pltpu.make_async_copy(o_v.at[:, at], qkv_ref.at[:, at], q_sem.at[j]),
-            pltpu.make_async_copy(buf.at[at], all_ref.at[at], h_sem.at[j]),
-        )
+        return pltpu.make_async_copy(h_v.at[at], h_ref.at[at], store_sem.at[j])
 
     def compute(j):
-        at = block_at(j, rows)
-        for i in range(3):
-
-            @pl.loop(0, width // TILE)
-            def _(t):
-                cols = block_at(t, TILE)
-                o_v[i, at, cols] = dot_nn(buf[at, :], w_v[i, :, cols]).astype(BF16)
-
-        for copy in stores(j):
-            copy.start()
-
-    load_w.wait()
+        @pl.loop(0, rows // CHUNK)
+        def _(i):
+            at = pl.ds(pl.multiple_of(j * rows + i * CHUNK, CHUNK), CHUNK)
+            hat, _ = normalize(buf[at, :].astype(F32))
+            h_v[at, :] = (hat * all_v[0:1, :] + all_v[2:3, :]).astype(BF16)
+
+        store(j).start()
+
     compute(p)
 
     @pl.loop(1, n)
@@ -311,37 +329,62 @@
             compute(p + s)
 
     gather.end()
+    store_n.wait()
+    for i in range(1, nd):
+        norm_copy(i, d).wait_send()
 
     @pl.loop(0, n)
     def _(j):
-        for copy in stores(j):
-            copy.wait()
-
-
-def project(normed, weights, n):
-    rows, model = normed.shape
-    width = weights.shape[2]
+        store(j).wait()
+
+
+def gather_rows(tokens, local_norms, n, nd):
+    rows, model = tokens.shape
     group = n * rows
     return remote_call(
-        functools.partial(project_kernel, n, rows),
-        "project",
+        functools.partial(gather_kernel, n, nd, rows),
+        "gather_rows",
         1,
-        (jax.ShapeDtypeStruct((3, group, width), BF16), jax.ShapeDtypeStruct((group, model), BF16)),
+        (jax.ShapeDtypeStruct((group, model), BF16), jax.ShapeDtypeStruct((8, model), F32)),
         [
             pltpu.VMEM((group, model), BF16),
-            pltpu.VMEM(weights.shape, BF16),
-            pltpu.VMEM((3, group, width), BF16),
+            pltpu.VMEM((group, model), BF16),
+            pltpu.VMEM((nd, 8, model // nd), F32),
+            pltpu.VMEM((8, model), F32),
             line_sems(n),
             line_sems(n),
             line_sems(n),
+            pltpu.SemaphoreType.DMA((nd,)),
+            pltpu.SemaphoreType.DMA((nd,)),
             pltpu.SemaphoreType.DMA((2,)),
             pltpu.SemaphoreType.DMA((n,)),
-            pltpu.SemaphoreType.DMA((n,)),
         ],
-        78,
-        normed,
-        weights,
-    )
+        75,
+        tokens,
+        local_norms,
+    )
+
+
+def project_kernel(h_ref, w_ref, out_ref):
+    out_ref[...] = dot_nn(h_ref[...], w_ref[...]).astype(BF16)
+
+
+def project(normed, weights):
+    group, model = normed.shape
+    width = weights.shape[2]
+    return pl.pallas_call(
+        project_kernel,
+        name="project",
+        out_shape=jax.ShapeDtypeStruct((3, group, width), BF16),
+        grid=(3, width // TILE),
+        in_specs=[
+            pl.BlockSpec((group, model), lambda i, t: (0, 0)),
+            pl.BlockSpec((pl.Squeezed(), model, TILE), lambda i, t: (i, 0, t)),
+        ],
+        out_specs=pl.BlockSpec((pl.Squeezed(), group, TILE), lambda i, t: (i, 0, t)),
+        cost_estimate=pl.CostEstimate(flops=int(1e10), bytes_accessed=1 << 23, transcendentals=0),
+        compiler_params=pltpu.CompilerParams(vmem_limit_bytes=VMEM_BYTES),
+    )(normed, weights)
 
 
 def branch_kernel(
@@ -986,13 +1029,17 @@
     return out[:4, :lanes]
 
 
+def low(values):
+    return lax.optimization_barrier(values.astype(BF16)).astype(F32)
+
+
 def per_device(tokens, w_qkv, w_out, w_up, w_down, norm_gains, norm_biases, lengths, cotangent):
     rows = tokens.shape[0]
     n, nd = lax.axis_size("tensor"), lax.axis_size("dp")
-    norms = lax.all_gather(
-        jnp.concatenate([norm_gains, norm_biases]).astype(BF16), "dp", axis=1, tiled=True
-    ).astype(F32)
-    gains, shifts = norms[:2], norms[2:]
+    local_norms = low(jnp.concatenate([norm_gains, norm_biases]))
+    local_norms = jnp.pad(local_norms, ((0, 4), (0, 0)))
+    normed_one_all, norms = gather_rows(tokens, local_norms, n, nd)
+    gains, shifts = norms[:2], norms[2:4]
     qkv_all = lax.all_gather(w_qkv.astype(BF16), "dp", axis=1, tiled=True)
     out_all = lax.all_gather(w_out.astype(BF16), "dp", axis=1, tiled=True)
     up_all = lax.all_gather(w_up.astype(BF16), "dp", axis=0, tiled=True)
@@ -1004,8 +1051,7 @@
     live_rows = (t * rows + jnp.arange(rows, dtype=jnp.int32) < lengths[0])[:, None]
     inputs = tokens.astype(F32)
     hat_one, inv_one = normalize(inputs)
-    normed_one = (hat_one * gains[0] + shifts[0]).astype(BF16)
-    qkv, normed_one_all = project(normed_one, qkv_all, n)
+    qkv = project(normed_one_all, qkv_all)
     attn, lse = attend(qkv, slopes, lengths)
     masked_cot = jnp.where(live_rows, cotangent, jnp.zeros_like(cotangent))
     attn_branch, masked_cot_all = branch(attn, out_all, masked_cot, n)
@@ -1020,10 +1066,13 @@
     d_after = masked_cot.astype(F32) + norm_back(d_norm_two, hat_two, inv_two, gains[1])
     d_branch = d_after.astype(BF16)
     grad_down = dot_tn(activated, masked_cot_all).astype(BF16)
-    down_shard = lax.psum_scatter(grad_down, "dp", scatter_dimension=1, tiled=True).astype(F32)
     grad_up = dot_tn(normed_two_all, d_up).astype(BF16)
-    up_shard = lax.psum_scatter(grad_up, "dp", scatter_dimension=0, tiled=True).astype(F32)
-    d_branch_all, d_attn, mlp_branch = unbranch(d_branch, out_all, mlp_part, n)
+    grad_down, grad_up, d_branch = lax.optimization_barrier((grad_down, grad_up, d_branch))
+    down_shard = lax.psum_scatter(grad_down, "dp", scatter_dimension=1, tiled=True)
+    up_shard = lax.psum_scatter(grad_up, "dp", scatter_dimension=0, tiled=True)
+    passed = unbranch(d_branch, out_all, mlp_part, n)
+    passed, down_shard, up_shard = lax.optimization_barrier((passed, down_shard, up_shard))
+    d_branch_all, d_attn, mlp_branch = passed
     output = jnp.where(live_rows, after_attn + mlp_branch, 0.0).astype(BF16)
     grad_out = dot_tn(attn, d_branch_all).astype(BF16)
     out_shard = lax.psum_scatter(grad_out, "dp", scatter_dimension=1, tiled=True).astype(F32)
@@ -1035,7 +1084,7 @@
     shift_one = jnp.sum(d_norm_one, axis=0)
     input_grad = (d_after + norm_back(d_norm_one, hat_one, inv_one, gains[0])).astype(BF16)
     sums = norm_sum(jnp.stack([gain_one, gain_two, shift_one, shift_two]), nd, n)
-    return (output, input_grad, qkv_shard, out_shard, up_shard, down_shard, sums[:2], sums[2:])
+    return (output, input_grad, qkv_shard, out_shard, up_shard.astype(F32), down_shard.astype(F32), sums[:2], sums[2:])
 
 
 def solution(mesh):

time: 798 us -> 711 us (0.89)
  waiting for transfers between devices: 109 us -> 20.4 us
  Pallas kernels: 563 us -> 578 us
  blocking collectives: 10.6 us -> 0 us
    reduce_scatter x1, waiting for transfers between devices: 72.3 us -> 19.7 us  [per_device(): up_shard = lax.psum_scatter(grad_up, 'dp', scatter_dimension=0, tiled=True)]
    all_gather x1, waiting for transfers between devices: 28.1 us -> 0.01 us  [per_device(): qkv_all = lax.all_gather(w_qkv.astype(BF16), 'dp', axis=1, tiled=True)]
    pallas_call x0 -> x1, Pallas kernels: none -> 11.9 us  [project(): pl.pallas_call(project_kernel, name='project', out_shape=jax.ShapeDtypeSt...]
    all_gather x1 -> x0, blocking collectives: 10.6 us -> none  [per_device(): lax.all_gather(jnp.concatenate([norm_gains, norm_biases]).astype(BF16), '...]
    reduce_scatter x1, waiting for transfers between devices: 8.08 us -> 0.02 us  [per_device(): lax.psum_scatter(grad_down, 'dp', scatter_dimension=1, tiled=True)]
  transfers between devices with their start and end apart: 8 -> 8, of which waited for: 3 -> 1; matrix products, arithmetic and copies ran while one was open for 9% -> 6% of each run, Pallas kernels for 42% -> 66%
where the time goes in v2:
time: 711 us; the launch traced here: 704 us
  Pallas kernels  578 us (81%)
  matrix products  41.5 us (6%)
  other arithmetic  38.1 us (5%)
  waiting for transfers between devices  20.4 us (3%)
  between operations  15.5 us (2%)
  local copies, waits for them, and re-layouts  9.83 us (1%)
    pallas_call x5, Pallas kernels, remote_call(): pl.pallas_call(body, name=name, out_shape=outs, in_specs=[ANY] * len(args...  509 us
    dot_general x6, matrix products, dot_tn(): lax.dot_general(left, right, (((0,), (0,)), ((), ())), preferred_element_...  41.5 us
    pallas_call x1, Pallas kernels, unattend(): pl.pallas_call(unattend_kernel, name='unattend', out_shape=jax.ShapeDtype...  23.2 us
    reduce_scatter x1, waiting for transfers between devices, per_device(): up_shard = lax.psum_scatter(grad_up, 'dp', scatter_dimension=0, tiled=True)  19.7 us
    pallas_call x1, Pallas kernels, norm_sum(): pl.pallas_call(functools.partial(norm_sum_kernel, nd, nt), name='norm_sum...  18.2 us
    pallas_call x1, Pallas kernels, attend(): pl.pallas_call(attend_kernel, name='attend', out_shape=(jax.ShapeDtypeStr...  15.7 us
  transfers between devices with their start and end apart: 8, of which 1 were waited for; matrix products, arithmetic and copies ran while one was open for 6% of the time, Pallas kernels for 66%

profile of v2, /device:TPU:0, one launch (start us, length us, event | category | flops | bytes accessed | tf_op | source)
XLA Modules:
  0.0 703.8 jit_solution(10981693680256320531)
XLA Ops:
  7.2 2.5 convert_element_type.63
  11.9 2.7 convert_element_type.67
  17.4 76.6 %gather_rows.1 = (bf16[1024,2048]{1,0:T(8,128)(2,1)}, f32[8,2048]{1,0:T(8,128)}) custom-call(bf16[256,2048]{1,0:T(8,128)(2,1)} %x_ref.1, f32[8,256]{1,0:T(8,128)} %pad_convert_fusion.nrm_ref), custom_call_target="tpu_custom_call" | custom-call | flops 86249996288 | bytes 1048576 | tf_op jit(solution)/shard_map/gather_rows/pallas_call | solution.py:248
  94.0 1.6 fusion.17
  97.3 11.9 %project.1.q_ref.k_ref.v_ref = bf16[3,1024,512]{2,1,0:T(8,128)(2,1)} custom-call(bf16[1024,2048]{1,0:T(8,128)(2,1)} %get-tuple-element.30.h_ref, bf16[3,2048,512]{2,1,0:T(8,128)(2,1)} %all-gather.5.cloned.1.call-done.w_ref), custom_call_target="tpu_custom_call" | custom-call | flops 10000000000 | bytes 8388608 | tf_op jit(solution)/shard_map/project/pallas_call | solution.py:375
  109.2 15.7 %attend.1 = (bf16[1024,512]{1,0:T(8,128)(2,1)}, f32[4,2,1024]{2,1,0:T(2,128)}) custom-call(s32[1]{0:T(128)} %copy.21.len_ref, f32[8]{0:T(128)} %multiply_exponential_fusion.slope_ref, bf16[3,1024,512]{2,1,0:T(8,128)(2,1)} %project.1.q_ref.k_ref.v_ref, bf16[3,1024,512]{2,1,0:T(8,128)(2,1)} %project.1.q_ref.k_ref.v_ref, ...), custom_call_target="tpu_custom_call" | custom-call | flops 20000000000 | bytes 4194304 | tf_op jit(solution)/shard_map/attend/pallas_call | solution.py:855
  125.0 121.1 %branch.1 = (f32[256,2048]{1,0:T(8,128)}, bf16[1024,2048]{1,0:T(8,128)(2,1)}) custom-call(bf16[1024,512]{1,0:T(8,128)(2,1)} %get-tuple-element.31.attn_ref, bf16[512,2048]{1,0:T(8,128)(2,1)} %all-gather.7.cloned.1.call-done.w_ref, bf16[256,2048]{1,0:T(8,128)(2,1)} %broadcast_select_fusion.g_ref), custom_call_target="tpu_custom_call" | custom-call | flops 115000000512 | bytes 1048576 | tf_op jit(solution)/shard_map/branch/pallas_call | solution.py:248
  246.1 2.8 fusion.16
  250.2 1.4 add_convert_fusion.h_ref
  251.6 115.4 %feed.1 = (bf16[1024,2048]{1,0:T(8,128)(2,1)}, bf16[1024,2048]{1,0:T(8,128)(2,1)}, bf16[1024,2048]{1,0:T(8,128)(2,1)}, bf16[1024,2048]{1,0:T(8,128)(2,1)}, f32[256,2048]{1,0:T(8,128)}) custom-call(bf16[256,2048]{1,0:T(8,128)(2,1)} %add_convert_fusion.h_ref, bf16[1024,2048]{1,0:T(8,128)(2,1)} %get-tuple-element.34.g_ref, ...), custom_call_target="tpu_custom_call" | custom-call | flops 160999997440 | bytes 1048576 | tf_op jit(solution)/shard_map/feed/pallas_call | solution.py:248
  367.0 14.2 %convolution_convert_fusion.1 = bf16[2048,2048]{1,0:T(8,128)(2,1)} fusion(bf16[1024,2048]{1,0:T(8,128)(2,1)} %get-tuple-element.35, bf16[1024,2048]{1,0:T(8,128)(2,1)} %get-tuple-element.34.g_ref), kind=kOutput, calls=%fused_computation.1 | convolution fusion | flops 8594128896 | bytes 16777216 | tf_op jit(solution)/shard_map/dot_general | solution.py:37
  381.3 2.6 multiply_reduce_fusion
  384.0 2.5 fusion.15
  387.1 1.5 copy-done.39
  388.6 11.4 %convolution_convert_fusion = bf16[2048,2048]{1,0:T(8,128)(2,1)} fusion(bf16[1024,2048]{1,0:T(8,128)(2,1)S(1)} %copy-done.38, bf16[1024,2048]{1,0:T(8,128)(2,1)S(1)} %copy-done.39), kind=kOutput, calls=%fused_computation | convolution fusion | flops 8594128896 | bytes 16777216 | tf_op jit(solution)/shard_map/dot_general | solution.py:37
  402.7 120.9 %unbranch.1 = (bf16[1024,2048]{1,0:T(8,128)(2,1)}, bf16[1024,512]{1,0:T(8,128)(2,1)}, f32[256,2048]{1,0:T(8,128)}) custom-call(bf16[256,2048]{1,0:T(8,128)(2,1)} %get-tuple-element.39.d_ref, bf16[512,2048]{1,0:T(8,128)(2,1)} %all-gather.7.cloned.1.call-done.w_ref, bf16[1024,2048]{1,0:T(8,128)(2,1)} %get-tuple-element.40.mlp_ref), custom_call_target="tpu_custom_call" | custom-call | flops 115000000512 | bytes 1048576 | tf_op jit(solution)/shard_map/unbranch/pallas_call | solution.py:248
  523.7 19.7 %reduce-scatter.7.cloned.1.call-done = bf16[256,2048]{1,0:T(8,128)(2,1)} async-done(((bf16[2048,2048]{1,0:T(8,128)(2,1)}), bf16[256,2048]{1,0:T(8,128)(2,1)}) %reduce-scatter.7.cloned.1.call-update) | async-done | bytes 1048592 | tf_op jit(solution)/shard_map/reduce_scatter | solution.py:1072
  543.4 5.9 convolution_convert_fusion.2
  549.4 23.2 %unattend.1.d_ref = bf16[3,1024,512]{2,1,0:T(8,128)(2,1)} custom-call(s32[1]{0:T(128)} %copy.21.len_ref, f32[8]{0:T(128)} %multiply_exponential_fusion.slope_ref, bf16[3,1024,512]{2,1,0:T(8,128)(2,1)} %project.1.q_ref.k_ref.v_ref, bf16[3,1024,512]{2,1,0:T(8,128)(2,1)} %project.1.q_ref.k_ref.v_ref, bf16[3,1024,512]{2,1,0:T(8,128)(2,1)} %project.1.q_ref.k_ref.v_ref, ...), custom_call_target="tpu_custom_call" | custom-call | flops 30000001024 | bytes 4194304 | tf_op jit(solution)/shard_map/unattend/pallas_call | solution.py:928
  572.6 5.0 fusion.2
  577.6 2.4 fusion.1
  580.1 2.4 fusion
  582.5 3.1 pad_maximum_fusion
  585.7 75.2 %unproject.1 = f32[256,2048]{1,0:T(8,128)} custom-call(bf16[3,1024,512]{2,1,0:T(8,128)(2,1)} %unattend.1.d_ref, bf16[3,2048,512]{2,1,0:T(8,128)(2,1)} %all-gather.5.cloned.1.call-done.w_ref), custom_call_target="tpu_custom_call" | custom-call | flops 92000002048 | bytes 1048576 | tf_op jit(solution)/shard_map/unproject/pallas_call | solution.py:248
  660.9 2.7 fusion.13
  664.6 18.2 %norm_sum.1 = f32[8,128]{1,0:T(8,128)} custom-call(f32[4,8,8,128]{3,2,1,0:T(8,128)} %pad.12.x_ref), custom_call_target="tpu_custom_call" | custom-call | tf_op jit(solution)/shard_map/norm_sum/pallas_call | solution.py:1012
  682.8 2.9 convert_element_type.77
  685.7 1.5 convert_element_type.78
  688.1 1.2 select_convert_fusion
  690.7 1.8 fusion.12
  692.5 1.8 convert_element_type.76
  694.3 2.5 convert_element_type.74
  (131 shorter events, 13.7 us)
Async XLA Ops:
  7.2 3.5 copy-start.11
  7.2 90.1 %all-gather.5.cloned.1.call-start = ((), (), s32[]{:S(2)}) async-start(), calls=%async_computation.4 | async-start | bytes 7077888 | tf_op jit(solution)/shard_map/all_gather | solution.py:1043
  9.8 115.2 %all-gather.7.cloned.1.call-start = ((), (), s32[]{:S(2)}) async-start(), calls=%async_computation.5 | async-start | bytes 2359296 | tf_op jit(solution)/shard_map/all_gather | solution.py:1044
  10.6 241.0 %all-gather.9.cloned.1.call-start = ((), (), s32[]{:S(2)}) async-start(), calls=%async_computation.6 | async-start | bytes 9437184 | tf_op jit(solution)/shard_map/all_gather | solution.py:1045
  11.8 4.2 copy-start.33
  11.8 4.2 copy-start.34
  11.8 4.2 copy-start.3
  11.8 239.8 %all-gather.11.cloned.1.call-start = ((), (), s32[]{:S(2)}) async-start(), calls=%async_computation.7 | async-start | bytes 9437184 | tf_op jit(solution)/shard_map/all_gather | solution.py:1046
  14.7 509.0 %reduce-scatter.5.cloned.1.call-start = ((), (), s32[]{:S(2)}) async-start(), calls=%async_computation.8 | async-start | bytes 9437184 | tf_op jit(solution)/shard_map/reduce_scatter | solution.py:1071
  17.4 78.8 %copy-start.9 = (bf16[256,2048]{1,0:T(8,128)(2,1)S(1)}, bf16[256,2048]{1,0:T(8,128)(2,1)}, u32[]{:S(2)}) copy-start(bf16[256,2048]{1,0:T(8,128)(2,1)} %param.17) | copy-start | bytes 3145732
  125.0 121.1 %copy-start.4 = (bf16[256,2048]{1,0:T(8,128)(2,1)S(1)}, bf16[256,2048]{1,0:T(8,128)(2,1)}, u32[]{:S(2)}) copy-start(bf16[256,2048]{1,0:T(8,128)(2,1)} %x_ref.1) | copy-start | bytes 3145732
  125.0 121.1 %copy-start.25 = (f32[256]{0:T(256)S(1)}, f32[256]{0:T(256)}, u32[]{:S(2)}) copy-start(f32[256]{0:T(256)} %broadcast_multiply_fusion.2) | copy-start | bytes 3076
  367.0 14.3 %copy-start.1 = (f32[256,2048]{1,0:T(8,128)S(1)}, f32[256,2048]{1,0:T(8,128)}, u32[]{:S(2)}) copy-start(f32[256,2048]{1,0:T(8,128)} %copy-done) | copy-start | bytes 6291460
  367.0 14.3 %copy-start.16 = (f32[1,2048]{1,0:T(1,128)S(1)}, f32[1,2048]{1,0:T(1,128)}, u32[]{:S(2)}) copy-start(f32[1,2048]{1,0:T(1,128)} %get-tuple-element.67) | copy-start | bytes 24580
  367.0 14.3 %copy-start.22 = (f32[256]{0:T(256)S(1)}, f32[256]{0:T(256)}, u32[]{:S(2)}) copy-start(f32[256]{0:T(256)} %copy-done.21) | copy-start | bytes 3076
  367.0 14.2 %copy-start.24 = (f32[256]{0:T(256)S(1)}, f32[256]{0:T(256)}, u32[]{:S(2)}) copy-start(f32[256]{0:T(256)} %copy-done.23) | copy-start | bytes 3076
  384.0 3.1 copy-start.38
  384.0 4.6 copy-start.39
  400.1 143.3 %reduce-scatter.7.cloned.1.call-start = ((), (), s32[]{:S(2)}) async-start(), calls=%async_computation.9 | async-start | bytes 9437184 | tf_op jit(solution)/shard_map/reduce_scatter | solution.py:1072
  400.7 291.8 %reduce-scatter.11.cloned.1.call-start = ((), (), s32[]{:S(2)}) async-start(), calls=%async_computation.11 | async-start | bytes 2359296 | tf_op jit(solution)/shard_map/reduce_scatter | solution.py:1078
  402.7 140.7 %copy-start.35 = (bf16[1024,512]{1,0:T(8,128)(2,1)S(1)}, bf16[1024,512]{1,0:T(8,128)(2,1)}, u32[]{:S(2)}) copy-start(bf16[1024,512]{1,0:T(8,128)(2,1)} %get-tuple-element.31.attn_ref) | copy-start | bytes 3145732
  549.3 144.9 %reduce-scatter.9.cloned.1.call-start = ((), (), s32[]{:S(2)}) async-start(), calls=%async_computation.10 | async-start | bytes 7077888 | tf_op jit(solution)/shard_map/reduce_scatter | solution.py:1081
  572.6 5.0 copy-start.36
  572.6 5.0 copy-start.37
  585.6 75.3 %copy-start.5 = (bf16[256,2048]{1,0:T(8,128)(2,1)S(1)}, bf16[256,2048]{1,0:T(8,128)(2,1)}, u32[]{:S(2)}) copy-start(bf16[256,2048]{1,0:T(8,128)(2,1)} %x_ref.1) | copy-start | bytes 3145732
  585.6 75.3 %copy-start.17 = (f32[1,2048]{1,0:T(1,128)S(1)}, f32[1,2048]{1,0:T(1,128)}, u32[]{:S(2)}) copy-start(f32[1,2048]{1,0:T(1,128)} %get-tuple-element.65) | copy-start | bytes 24580
  585.7 75.3 %copy-start.26 = (f32[256]{0:T(256)S(1)}, f32[256]{0:T(256)}, u32[]{:S(2)}) copy-start(f32[256]{0:T(256)} %broadcast_multiply_fusion.2) | copy-start | bytes 3076
  585.7 75.3 %copy-start.28 = (f32[256]{0:T(256)S(1)}, f32[256]{0:T(256)}, u32[]{:S(2)}) copy-start(f32[256]{0:T(256)} %add_rsqrt_fusion) | copy-start | bytes 3076
  660.9 3.0 copy-start.18
  660.9 3.0 copy-start.19
  660.9 26.9 %copy-start.12 = (f32[256,2048]{1,0:T(8,128)S(1)}, f32[256,2048]{1,0:T(8,128)}, u32[]{:S(2)}) copy-start(f32[256,2048]{1,0:T(8,128)} %get-tuple-element.46) | copy-start | bytes 6291460
  682.8 2.9 copy-start.13
  (16 other events, 28.8 us)
Sparse Core Ops, SparseCore 0:
  10.5 48.4 all-gather.4
  61.4 28.0 all-gather.6
  92.0 54.2 all-gather.8
  148.6 55.8 all-gather.10
  400.2 68.3 reduce-scatter.4
  471.9 71.4 reduce-scatter.6
  549.5 41.0 reduce-scatter.10
  593.9 61.6 reduce-scatter.8
